TPU v7x, 32 devices: a whole 2x2x4 slice. The times are simulated.
32 devices in a mesh: px: 4 (over x, core), py: 8 (over z, y).
Axes of the slice: x: 2, y: 2, z: 4, core: 2. Of those that a mesh axis runs over, the one named last changes fastest.
Arguments:
- root_density: float32 [384, 384, 384], P('px', 'py'), may hold values from -6 to 6
- subgrid_density: float32 [256, 32, 1024], P(('px', 'py')), may hold values from -24 to 24
- velocity: float32 [3, 256, 32, 1024], P(None, ('px', 'py')), may hold values from -6 to 6
- slot_anchor: int32 [3, 256], replicated, may hold values from 0 to 376, as said below
- slot_count: int32 [32], replicated, may hold values from 1 to 8, as said below
- neighbour: int32 [2, 256], replicated, may hold values from -1 to 255, as said below
Outputs:
- coarse_potential: float32 [384, 384, 384], P('px', 'py')
- subgrid_potential: float32 [256, 32, 1024], P(('px', 'py'))
- kicked_velocity: float32 [3, 256, 32, 1024], P(None, ('px', 'py'))
Inputs may be any that keep to these rules, and one draw needn't show every extreme that they name: Slot j of device d is slot d * 8 + j, devices numbered in the order of px+py; it is live when j < slot_count[d]. Some device has every slot live. `slot_anchor`: entries are multiples of 8; live slots cover distinct regions of 8^3 root cells; empty slots hold 0. The region of live slot j of the device at px = p, py = q has its lower corner among the root cells that the device at px = p, py = (q + j) mod 8 holds of root_density. neighbour[0, s] is s - 8 or -1 and neighbour[1, s] is s + 8 or -1, the same slot of the device one index lower or higher along py with the same px; where set, both slots are live and the two regions lie next to each other along the second dimension, the lower one below. Empty slots hold -1.
All inputs are finite; a program needn't handle non-finite values.
Results may differ from a plain program's by a relative error of at most 0.000094.
Values sent between devices are 32-bit elements; how exact they have to be, the bound alone decides.
A program may use at most 192 MiB of HBM per device.

v0:
```python
import jax
import jax.numpy as jnp
from jax import lax
from jax.sharding import PartitionSpec as P

NR = 384
REG = 8
REF = 4
SWEEPS = 4


HIGHEST_PRECISION = lax.Precision.HIGHEST
RELAXATION = 6.0 / 7.0
EINSUM_FORMS = ("abc,ad->dbc", "abc,bd->adc", "abc,cd->abd")


def from_behind(value, axis, steps):
    count = lax.axis_size(axis)
    initial, last = (max(0, -steps), min(count, count - steps))
    return lax.ppermute(value, axis, [(source, source + steps) for source in range(initial, last)])


def extended(block, sides, width):
    for axis, dim in sides:
        count = lax.axis_size(axis)
        forward = [(i, i + 1) for i in range(count - 1)]
        forward.append((count - 1, 0))
        backward = [(target, source) for source, target in forward]
        low = lax.ppermute(
            lax.slice_in_dim(block, block.shape[dim] - width, None, axis=dim), axis, forward
        )
        high = lax.ppermute(lax.slice_in_dim(block, 0, width, axis=dim), axis, backward)
        block = jnp.concatenate([low, block, high], axis=dim)
    return block


def tables(length):
    positions = jnp.arange(length, dtype=jnp.int32)
    angle_table = (
        2.0
        * jnp.pi
        / length
        * (positions[:, None] * positions[None, :] % length).astype(jnp.float32)
    )
    return (jnp.cos(angle_table), jnp.sin(angle_table))


def transform_along(values_in, matrix, axis_number):
    return jnp.einsum(EINSUM_FORMS[axis_number], values_in, matrix, precision=HIGHEST_PRECISION)


def forward(complex_pair, axis_number, cosine_table, sine_table):
    real_part, imag_part = complex_pair
    return (
        transform_along(real_part, cosine_table, axis_number)
        + transform_along(imag_part, sine_table, axis_number),
        transform_along(imag_part, cosine_table, axis_number)
        - transform_along(real_part, sine_table, axis_number),
    )


def inverse(complex_pair, axis_number, cosine_table, sine_table):
    real_part, imag_part = complex_pair
    scale_factor = 1.0 / cosine_table.shape[0]
    return (
        (
            transform_along(real_part, cosine_table, axis_number)
            - transform_along(imag_part, sine_table, axis_number)
        )
        * scale_factor,
        (
            transform_along(imag_part, cosine_table, axis_number)
            + transform_along(real_part, sine_table, axis_number)
        )
        * scale_factor,
    )


def eigenvalue(wavenumber):
    return -4.0 * jnp.sin(jnp.pi / NR * wavenumber.astype(jnp.float32)) ** 2


def green_block(wave_first, wave_second, wave_third):
    total = (
        eigenvalue(wave_first)[:, None, None]
        + eigenvalue(wave_second)[None, :, None]
        + eigenvalue(wave_third)[None, None, :]
    )
    zero_mode = (
        (wave_first[:, None, None] == 0)
        & (wave_second[None, :, None] == 0)
        & (wave_third[None, None, :] == 0)
    )
    safe_total = jnp.where(zero_mode, -1.0, total)
    return jnp.where(zero_mode, 0.0, 1.0 / safe_total)


def weights_table():
    cells = jnp.arange(REG * REF + 2, dtype=jnp.int32)
    marks = 2 * cells - 1 + REF
    lower_cell = jnp.minimum(marks // (2 * REF), REG)
    fraction = (marks - 2 * REF * lower_cell).astype(jnp.float32) / (2 * REF)
    columns = jnp.arange(REG + 2, dtype=jnp.int32)
    return jnp.where(
        columns[None, :] == lower_cell[:, None], 1.0 - fraction[:, None], 0.0
    ) + jnp.where(columns[None, :] == lower_cell[:, None] + 1, fraction[:, None], 0.0)


def coarse_parts(patch_flat, weights):
    inner = weights[1:-1]
    cells = inner.shape[0]
    width = weights.shape[1]
    both_inner = jnp.einsum("jb,kc->jkbc", inner, inner, precision=HIGHEST_PRECISION).reshape(
        cells * cells, width * width
    )
    second_low = jnp.einsum("b,kc->kbc", weights[0], inner, precision=HIGHEST_PRECISION).reshape(
        cells, width * width
    )
    second_high = jnp.einsum("b,kc->kbc", weights[-1], inner, precision=HIGHEST_PRECISION).reshape(
        cells, width * width
    )
    third_low = jnp.einsum("jb,c->jbc", inner, weights[0], precision=HIGHEST_PRECISION).reshape(
        cells, width * width
    )
    third_high = jnp.einsum("jb,c->jbc", inner, weights[-1], precision=HIGHEST_PRECISION).reshape(
        cells, width * width
    )
    plane_values = jnp.einsum("sam,nm->san", patch_flat, both_inner, precision=HIGHEST_PRECISION)
    interior = jnp.einsum("san,ia->sin", plane_values, inner, precision=HIGHEST_PRECISION)
    first_low_face = jnp.einsum("san,a->sn", plane_values, weights[0], precision=HIGHEST_PRECISION)
    first_high_face = jnp.einsum(
        "san,a->sn", plane_values, weights[-1], precision=HIGHEST_PRECISION
    )

    def face_of(table):
        partial_face = jnp.einsum("sam,km->sak", patch_flat, table, precision=HIGHEST_PRECISION)
        return jnp.einsum("sak,ia->sik", partial_face, inner, precision=HIGHEST_PRECISION)

    return (
        interior,
        first_low_face,
        first_high_face,
        face_of(second_low),
        face_of(second_high),
        face_of(third_low),
        face_of(third_high),
    )


def spread_third(face_values, cells, corner):
    positions = jnp.arange(cells * cells, dtype=jnp.int32)
    rows = jnp.arange(cells, dtype=jnp.int32)
    placer = (positions[None, :] == rows[:, None] * cells + corner).astype(jnp.float32)
    return jnp.einsum("sij,jn->sin", face_values, placer, precision=HIGHEST_PRECISION)


def beside_values(interior, first_faces, second_faces, third_full, third_place):
    cells = interior.shape[1]
    slots = interior.shape[0]
    first_low, first_high = first_faces
    second_low, second_high = second_faces
    third_low, third_high = third_full
    below_first = jnp.concatenate([first_low[:, None, :], interior[:, :-1]], axis=1)
    above_first = jnp.concatenate([interior[:, 1:], first_high[:, None, :]], axis=1)
    below_second = jnp.concatenate([second_low, interior[:, :, :-cells]], axis=2)
    above_second = jnp.concatenate([interior[:, :, cells:], second_high], axis=2)
    zero_column = jnp.zeros((slots, cells, 1), jnp.float32)
    below_third = jnp.where(
        third_place == 0, third_low, jnp.concatenate([zero_column, interior[:, :, :-1]], axis=2)
    )
    above_third = jnp.where(
        third_place == cells - 1,
        third_high,
        jnp.concatenate([interior[:, :, 1:], zero_column], axis=2),
    )
    return ((below_first, above_first), (below_second, above_second), (below_third, above_third))


def cut_patches(padded, anchors, corner_first, corner_second):
    offsets = jnp.arange(REG + 2, dtype=jnp.int32)
    index_first = jnp.clip(
        anchors[0][:, None] - corner_first + offsets[None, :], 0, padded.shape[0] - 1
    )
    index_second = jnp.clip(
        anchors[1][:, None] - corner_second + offsets[None, :], 0, padded.shape[1] - 1
    )
    index_third = (anchors[2][:, None] - 1 + offsets[None, :]) % NR
    picked = padded[
        index_first[:, :, None, None], index_second[:, None, :, None], index_third[:, None, None, :]
    ]
    return picked.reshape(anchors.shape[1], -1)


def neighbour_faces(interior):
    cells = interior.shape[1]
    top_layer = interior[:, :, (cells - 1) * cells :]
    bottom_layer = interior[:, :, :cells]
    from_below = from_behind(top_layer, "py", 1)
    from_above = from_behind(bottom_layer, "py", -1)
    return (from_below, from_above)


def local(root_density, subgrid_density, velocity, slot_anchor, slot_count, neighbour):
    cosine_table, sine_table = tables(NR)
    first_rows = root_density.shape[0]
    second_rows = root_density.shape[1]
    size_second = lax.axis_size("py")
    place_first = lax.axis_index("px")
    place_second = lax.axis_index("py")
    device = place_first * size_second + place_second
    every_wave = jnp.arange(NR, dtype=jnp.int32)
    real_part = transform_along(root_density, cosine_table, 2)
    imag_part = -transform_along(root_density, sine_table, 2)
    spectrum = (
        lax.all_to_all(real_part, "py", split_axis=0, concat_axis=1, tiled=True),
        lax.all_to_all(imag_part, "py", split_axis=0, concat_axis=1, tiled=True),
    )
    spectrum = forward(spectrum, 1, cosine_table, sine_table)
    spectrum = (
        lax.all_to_all(spectrum[0], ("px", "py"), split_axis=1, concat_axis=0, tiled=True),
        lax.all_to_all(spectrum[1], ("px", "py"), split_axis=1, concat_axis=0, tiled=True),
    )
    band = spectrum[0].shape[1]
    band_start = device * band
    spectrum = forward(spectrum, 0, cosine_table, sine_table)
    factor = green_block(every_wave, band_start + jnp.arange(band, dtype=jnp.int32), every_wave)
    spectrum = inverse((spectrum[0] * factor, spectrum[1] * factor), 0, cosine_table, sine_table)
    spectrum = (
        lax.all_to_all(spectrum[0], ("px", "py"), split_axis=0, concat_axis=1, tiled=True),
        lax.all_to_all(spectrum[1], ("px", "py"), split_axis=0, concat_axis=1, tiled=True),
    )
    spectrum = inverse(spectrum, 1, cosine_table, sine_table)
    spectrum = (
        lax.all_to_all(spectrum[0], "py", split_axis=1, concat_axis=0, tiled=True),
        lax.all_to_all(spectrum[1], "py", split_axis=1, concat_axis=0, tiled=True),
    )
    coarse_potential = (
        transform_along(spectrum[0], cosine_table, 2) - transform_along(spectrum[1], sine_table, 2)
    ) * (1.0 / NR)
    per_device = subgrid_density.shape[0]
    cells = subgrid_density.shape[1]
    positions = jnp.arange(per_device, dtype=jnp.int32)
    corner_first = place_first * first_rows
    corner_second = place_second * second_rows
    padded = extended(coarse_potential, (("px", 0), ("py", 1)), 1)
    targets = jnp.arange(size_second, dtype=jnp.int32)
    owner_devices = place_first * size_second + targets
    wanted_slot = (place_second - targets) % size_second
    global_slot = owner_devices * per_device + wanted_slot
    sending_live = wanted_slot < slot_count[owner_devices]
    sending = cut_patches(padded, slot_anchor[:, global_slot], corner_first, corner_second)
    sending = jnp.where(sending_live[:, None], sending, 0.0)
    arrived = lax.all_to_all(sending, "py", split_axis=0, concat_axis=0, tiled=True)
    patch = arrived[(place_second + positions) % size_second]
    patch_flat = patch.reshape(per_device, REG + 2, (REG + 2) * (REG + 2))
    interior, first_low, first_high, second_low, second_high, third_low, third_high = coarse_parts(
        patch_flat, weights_table()
    )
    third_full = (spread_third(third_low, cells, 0), spread_third(third_high, cells, cells - 1))
    third_place = jnp.arange(cells * cells, dtype=jnp.int32) % cells
    own_live = positions < slot_count[device]
    first_slot = device * per_device
    nearby = lax.dynamic_slice_in_dim(neighbour, first_slot, per_device, 1)
    use_below = (nearby[0] >= 0)[:, None, None]
    use_above = (nearby[1] >= 0)[:, None, None]

    def all_beside(current):
        from_below, from_above = neighbour_faces(current)
        second_faces = (
            jnp.where(use_below, from_below, second_low),
            jnp.where(use_above, from_above, second_high),
        )
        return beside_values(
            current, (first_low, first_high), second_faces, third_full, third_place
        )

    for sweep_index in range(SWEEPS):
        along_first, along_second, along_third = all_beside(interior)
        beside_all = (
            along_first[1]
            + along_first[0]
            + along_second[1]
            + along_second[0]
            + along_third[1]
            + along_third[0]
        )
        interior = (1.0 - RELAXATION) * interior + RELAXATION * (
            beside_all - subgrid_density * (1.0 / (REF * REF))
        ) / 6.0
    along_first, along_second, along_third = all_beside(interior)
    scale_factor = REF / 2.0
    slopes = jnp.stack(
        [
            (along_first[1] - along_first[0]) * scale_factor,
            (along_second[1] - along_second[0]) * scale_factor,
            (along_third[1] - along_third[0]) * scale_factor,
        ]
    )
    subgrid_potential = jnp.where(own_live[:, None, None], interior, 0.0)
    velocity_after_kick = jnp.where(own_live[None, :, None, None], velocity - slopes, 0.0)
    return (coarse_potential, subgrid_potential, velocity_after_kick)


def solution(mesh):
    return jax.shard_map(
        local,
        mesh=mesh,
        in_specs=(
            P("px", "py", None),
            P(("px", "py"), None, None),
            P(None, ("px", "py"), None, None),
            P(),
            P(),
            P(),
        ),
        out_specs=(
            P("px", "py", None),
            P(("px", "py"), None, None),
            P(None, ("px", "py"), None, None),
        ),
        check_vma=False,
    )
```

profile of v0, /device:TPU:5, one launch (start us, length us, event | category | flops | bytes accessed | tf_op | source)
XLA Modules:
  0.0 2282.8 jit_solution(2776538511721893047)
XLA Ops:
  0.6 21.9 negate_bitcast_fusion
  35.3 22.0 fusion.6
  64.4 125.3 %all-to-all-done.1 = f32[96,48,384]{2,1,0:T(8,128)} async-done(((f32[96,48,384]{2,1,0:T(8,128)}), f32[96,48,384]{2,1,0:T(8,128)}, u32[]{:S(2)}, u32[]{:S(2)}) %all-to-all-start.1) | async-done | bytes 7077920 | tf_op jit(solution)/shard_map/all_to_all | solution.py:216
  201.1 147.7 %all-to-all-done = f32[96,48,384]{2,1,0:T(8,128)} async-done(((f32[96,48,384]{2,1,0:T(8,128)}), f32[96,48,384]{2,1,0:T(8,128)}, u32[]{:S(2)}, u32[]{:S(2)}) %all-to-all-start) | async-done | bytes 7077920 | tf_op jit(solution)/shard_map/all_to_all | solution.py:215
  352.6 13.9 fusion.66
  366.5 13.9 add_bitcast_fusion
  393.8 19.1 fusion.61
  412.9 18.8 subtract_bitcast_fusion
  439.6 160.5 %all-to-all-done.2 = f32[12,384,384]{2,0,1:T(8,128)} async-done(((f32[12,384,384]{2,0,1:T(8,128)}), f32[12,384,384]{2,0,1:T(8,128)}, u32[]{:S(2)}, u32[]{:S(2)}) %all-to-all-start.2) | async-done | bytes 7077920 | tf_op jit(solution)/shard_map/all_to_all | solution.py:220
  627.2 189.0 %all-to-all-done.3 = f32[12,384,384]{2,0,1:T(8,128)} async-done(((f32[12,384,384]{2,0,1:T(8,128)}), f32[12,384,384]{2,0,1:T(8,128)}, u32[]{:S(2)}, u32[]{:S(2)}) %all-to-all-start.3) | async-done | bytes 7077920 | tf_op jit(solution)/shard_map/all_to_all | solution.py:221
  833.5 21.8 fusion.59
  855.3 14.7 fusion.68
  870.0 19.8 subtract_multiply_fusion.2
  889.9 17.1 add_multiply_fusion.1
  907.0 14.7 fusion.57
  921.7 15.2 add_multiply_fusion
  954.5 19.1 fusion.70
  973.6 18.9 subtract_multiply_fusion.1
  1000.3 160.7 %all-to-all-done.5 = f32[384,12,384]{2,1,0:T(8,128)} async-done(((f32[384,12,384]{2,1,0:T(8,128)}), f32[384,12,384]{2,1,0:T(8,128)}, u32[]{:S(2)}, u32[]{:S(2)}) %all-to-all-start.5) | async-done | bytes 7077920 | tf_op jit(solution)/shard_map/all_to_all | solution.py:230
  1161.0 10.0 all-to-all-start.4
  1188.3 189.1 %all-to-all-done.4 = f32[384,12,384]{2,1,0:T(8,128)} async-done(((f32[384,12,384]{2,1,0:T(8,128)}), f32[384,12,384]{2,1,0:T(8,128)}, u32[]{:S(2)}, u32[]{:S(2)}) %all-to-all-start.4) | async-done | bytes 7077920 | tf_op jit(solution)/shard_map/all_to_all | solution.py:229
  1394.5 18.4 fusion.55
  1412.9 14.2 multiply_bitcast_fusion
  1434.9 10.9 all-to-all-start.7
  1445.8 19.1 fusion.72
  1465.0 19.1 multiply_bitcast_fusion.1
  1491.9 158.8 %all-to-all-done.7 = f32[12,384,384]{2,0,1:T(8,128)} async-done(((f32[12,384,384]{2,0,1:T(8,128)}), f32[12,384,384]{2,0,1:T(8,128)}, u32[]{:S(2)}, u32[]{:S(2)}) %all-to-all-start.7) | async-done | bytes 7077920 | tf_op jit(solution)/shard_map/all_to_all | solution.py:235
  1671.0 189.8 %all-to-all-done.6 = f32[12,384,384]{2,0,1:T(8,128)} async-done(((f32[12,384,384]{2,0,1:T(8,128)}), f32[12,384,384]{2,0,1:T(8,128)}, u32[]{:S(2)}, u32[]{:S(2)}) %all-to-all-start.6) | async-done | bytes 7077920 | tf_op jit(solution)/shard_map/all_to_all | solution.py:234
  1866.6 20.1 fusion.63
  1886.7 17.8 subtract_multiply_fusion
  1926.9 254.5 %gather_fusion.2 = f32[8000]{0:T(1024)S(1)} fusion(f32[98,50,384]{2,1,0:T(8,128)} %pad_maximum_fusion, s32[8000]{0:T(1024)S(1)} %reshape.573), kind=kCustom, calls=%fused_computation.2 | custom fusion | bytes 160000 | tf_op jit(solution)/shard_map/gather | solution.py:188
  2182.2 26.4 %all-to-all-start.8 = ((f32[8,1,1000]{2,1,0:T(1,128)}), f32[8,1,1000]{2,1,0:T(1,128)S(1)}, u32[]{:S(2)}, u32[]{:S(2)}) async-start(f32[8,1,1000]{2,1,0:T(1,128)} %broadcast_select_fusion.1), calls=%async_computation.8 | async-start | bytes 65536 | tf_op jit(solution)/shard_map/all_to_all | solution.py:253
  (232 shorter events, 298.4 us)
Async XLA Ops:
  0.6 1656.8 %copy-start = (s32[2,256]{1,0:T(2,128)S(1)}, s32[2,256]{1,0:T(2,128)}, u32[]{:S(2)}) copy-start(s32[2,256]{1,0:T(2,128)} %param.11) | copy-start | bytes 6148
  29.5 160.1 %all-to-all-start.1 = ((f32[96,48,384]{2,1,0:T(8,128)}), f32[96,48,384]{2,1,0:T(8,128)}, u32[]{:S(2)}, u32[]{:S(2)}) async-start(f32[96,48,384]{2,1,0:T(8,128)} %copy.89), calls=%async_computation.1 | async-start | bytes 14155776 | tf_op jit(solution)/shard_map/all_to_all | solution.py:216
  189.7 159.1 %all-to-all-start = ((f32[96,48,384]{2,1,0:T(8,128)}), f32[96,48,384]{2,1,0:T(8,128)}, u32[]{:S(2)}, u32[]{:S(2)}) async-start(f32[96,48,384]{2,1,0:T(8,128)} %copy.85), calls=%async_computation | async-start | bytes 14155776 | tf_op jit(solution)/shard_map/all_to_all | solution.py:215
  388.2 211.9 %all-to-all-start.2 = ((f32[12,384,384]{2,0,1:T(8,128)}), f32[12,384,384]{2,0,1:T(8,128)}, u32[]{:S(2)}, u32[]{:S(2)}) async-start(f32[12,384,384]{2,0,1:T(8,128)} %copy.92), calls=%async_computation.2 | async-start | bytes 18874368 | tf_op jit(solution)/shard_map/all_to_all | solution.py:220
  600.1 216.1 %all-to-all-start.3 = ((f32[12,384,384]{2,0,1:T(8,128)}), f32[12,384,384]{2,0,1:T(8,128)}, u32[]{:S(2)}, u32[]{:S(2)}) async-start(f32[12,384,384]{2,0,1:T(8,128)} %copy.98), calls=%async_computation.3 | async-start | bytes 18874368 | tf_op jit(solution)/shard_map/all_to_all | solution.py:221
  944.8 216.2 %all-to-all-start.5 = ((f32[384,12,384]{2,1,0:T(8,128)}), f32[384,12,384]{2,1,0:T(8,128)}, u32[]{:S(2)}, u32[]{:S(2)}) async-start(f32[384,12,384]{2,1,0:T(8,128)} %copy.112), calls=%async_computation.5 | async-start | bytes 18874368 | tf_op jit(solution)/shard_map/all_to_all | solution.py:230
  1161.0 216.4 %all-to-all-start.4 = ((f32[384,12,384]{2,1,0:T(8,128)}), f32[384,12,384]{2,1,0:T(8,128)}, u32[]{:S(2)}, u32[]{:S(2)}) async-start(f32[384,12,384]{2,1,0:T(8,128)} %copy.106), calls=%async_computation.4 | async-start | bytes 18874368 | tf_op jit(solution)/shard_map/all_to_all | solution.py:229
  1434.9 215.8 %all-to-all-start.7 = ((f32[12,384,384]{2,0,1:T(8,128)}), f32[12,384,384]{2,0,1:T(8,128)}, u32[]{:S(2)}, u32[]{:S(2)}) async-start(f32[12,384,384]{2,0,1:T(8,128)} %copy.120), calls=%async_computation.7 | async-start | bytes 18874368 | tf_op jit(solution)/shard_map/all_to_all | solution.py:235
  1650.7 210.1 %all-to-all-start.6 = ((f32[12,384,384]{2,0,1:T(8,128)}), f32[12,384,384]{2,0,1:T(8,128)}, u32[]{:S(2)}, u32[]{:S(2)}) async-start(f32[12,384,384]{2,0,1:T(8,128)} %copy.116), calls=%async_computation.6 | async-start | bytes 18874368 | tf_op jit(solution)/shard_map/all_to_all | solution.py:234
  1904.6 3.6 collective-permute-start
  1906.8 3.8 collective-permute-start.1
  1910.7 8.7 collective-permute-start.2
  1910.8 8.6 collective-permute-start.3
  1926.8 282.5 %copy-start.18 = (f32[32,10,10]{0,1,2:T(8,128)S(1)}, f32[32,10,10]{0,1,2:T(8,128)}, u32[]{:S(2)}) copy-start(f32[32,10,10]{0,1,2:T(8,128)} %get-tuple-element.62) | copy-start | bytes 38404
  1926.8 282.5 %copy-start.17 = (f32[32,10,10]{0,2,1:T(8,128)S(1)}, f32[32,10,10]{0,2,1:T(8,128)}, u32[]{:S(2)}) copy-start(f32[32,10,10]{0,2,1:T(8,128)} %get-tuple-element.63) | copy-start | bytes 38404
  1926.8 282.5 %copy-start.16 = (f32[32,10,10]{0,2,1:T(8,128)S(1)}, f32[32,10,10]{0,2,1:T(8,128)}, u32[]{:S(2)}) copy-start(f32[32,10,10]{0,2,1:T(8,128)} %get-tuple-element.66) | copy-start | bytes 38404
  1926.8 282.5 %copy-start.15 = (f32[32,10,10]{0,1,2:T(8,128)S(1)}, f32[32,10,10]{0,1,2:T(8,128)}, u32[]{:S(2)}) copy-start(f32[32,10,10]{0,1,2:T(8,128)} %get-tuple-element.67) | copy-start | bytes 38404
  1926.8 282.6 %copy-start.11 = (f32[32,32,10,10]{1,0,3,2:T(8,128)S(1)}, f32[32,32,10,10]{1,0,3,2:T(8,128)}, u32[]{:S(2)}) copy-start(f32[32,32,10,10]{1,0,3,2:T(8,128)} %multiply_bitcast_fusion.2) | copy-start | bytes 1228804
  1926.8 287.3 %copy-start.26 = (f32[10]{0:T(128)S(1)}, f32[10]{0:T(128)}, u32[]{:S(2)}) copy-start(f32[10]{0:T(128)} %copy-done.25) | copy-start | bytes 124
  1926.9 287.8 %copy-start.24 = (f32[10]{0:T(128)S(1)}, f32[10]{0:T(128)}, u32[]{:S(2)}) copy-start(f32[10]{0:T(128)} %copy-done.23) | copy-start | bytes 124
  1926.9 288.2 %copy-start.14 = (f32[34,10]{0,1:T(8,128)S(1)}, f32[34,10]{0,1:T(8,128)}, u32[]{:S(2)}) copy-start(f32[34,10]{0,1:T(8,128)} %copy-done.13) | copy-start | bytes 4084
  2182.2 30.6 %all-to-all-start.8 = ((f32[8,1,1000]{2,1,0:T(1,128)}), f32[8,1,1000]{2,1,0:T(1,128)S(1)}, u32[]{:S(2)}, u32[]{:S(2)}) async-start(f32[8,1,1000]{2,1,0:T(1,128)} %broadcast_select_fusion.1), calls=%async_computation.8 | async-start | bytes 65536 | tf_op jit(solution)/shard_map/all_to_all | solution.py:253
  2218.8 7.2 collective-permute-start.4
  2223.0 5.7 collective-permute-start.5
  2231.3 7.0 collective-permute-start.7
  2235.6 6.6 collective-permute-start.6
  2244.7 6.7 collective-permute-start.8
  2246.8 6.2 collective-permute-start.9
  2255.4 7.1 collective-permute-start.10
  2257.7 6.6 collective-permute-start.11
  2268.0 7.7 collective-permute-start.13
  2272.9 6.6 collective-permute-start.12
  (26 other events, 918.0 us)
where the time goes:
time: 2300 us; the launch traced here: 2280 us
  waiting for transfers between devices  1350 us (59%)
  local copies, waits for them, and re-layouts  419 us (18%)
  matrix products  367 us (16%)
  starting transfers between devices  123 us (5%)
  other arithmetic  25.4 us (1%)
    dot_general x20, matrix products, transform_along(): jnp.einsum(EINSUM_FORMS[axis_number], values_in, matrix, precision=HIGHES...  360 us
    gather x1, local copies, waits for them, and re-layouts, cut_patches(): padded[index_first[:, :, None, None], index_second[:, None, :, None], ind...  254 us
    all_to_all x1, waiting for transfers between devices, local(): lax.all_to_all(spectrum[0], 'py', split_axis=1, concat_axis=0, tiled=True)  190 us
    all_to_all x1, waiting for transfers between devices, local(): lax.all_to_all(spectrum[0], ('px', 'py'), split_axis=0, concat_axis=1, ti...  189 us
    all_to_all x1, waiting for transfers between devices, local(): lax.all_to_all(spectrum[1], ('px', 'py'), split_axis=1, concat_axis=0, ti...  189 us
    all_to_all x1, waiting for transfers between devices, local(): lax.all_to_all(spectrum[1], ('px', 'py'), split_axis=0, concat_axis=1, ti...  161 us
    all_to_all x1, waiting for transfers between devices, local(): lax.all_to_all(spectrum[0], ('px', 'py'), split_axis=1, concat_axis=0, ti...  161 us
    all_to_all x1, waiting for transfers between devices, local(): lax.all_to_all(spectrum[1], 'py', split_axis=1, concat_axis=0, tiled=True)  159 us
  transfers between devices with their start and end apart: 23, of which 19 were waited for; matrix products, arithmetic and copies ran while one was open for 9% of the time, Pallas kernels for 0%

commit v1 on v0

v1 whole, which is shorter than its diff:
```python
import jax
import jax.numpy as jnp
import numpy as np
from jax import lax
from jax.experimental import pallas as pl
from jax.experimental.pallas import tpu as pltpu
from jax.sharding import PartitionSpec as P

NR = 384
REG = 8
REF = 4
SWEEPS = 4
CELLS = REG * REF
EDGE = SWEEPS
LAYERS = CELLS + 2 * EDGE
WIDE = LAYERS * CELLS
RELAXATION = 6.0 / 7.0
HIGHEST = lax.Precision.HIGHEST
HIGH = lax.Precision.HIGH
F32 = jnp.float32


def fourier_basis(length):
    cell = np.arange(length)
    rows = []
    for k in range(length):
        if k in (0, length // 2):
            rows.append(np.cos(2 * np.pi * (k * cell % length) / length) / np.sqrt(length))
        elif k < length // 2:
            rows.append(np.cos(2 * np.pi * (k * cell % length) / length) * np.sqrt(2 / length))
        else:
            rows.append(
                np.sin(2 * np.pi * ((length - k) * cell % length) / length) * np.sqrt(2 / length)
            )
    return np.stack(rows)


def pseudo_inverse(length):
    basis = fourier_basis(length)
    eig = -4 * np.sin(np.pi * np.arange(length) / length) ** 2
    scale = np.where(np.arange(length) == 0, 0.0, 1 / np.where(eig == 0, -1.0, eig))
    return (basis.T * scale) @ basis


def axis_weights(cells, first, count):
    table = np.zeros((len(cells), count))
    for row, cell in enumerate(cells):
        mark = 2 * cell - 1 + REF
        low = mark // (2 * REF)
        frac = (mark - 2 * REF * low) / (2 * REF)
        table[row, low - first] += 1 - frac
        if frac:
            table[row, low + 1 - first] += frac
    return table


PATCH_X = REG + 2
PATCH_Y = REG + 4
PATCH_Z = REG + 2


def patch_tables():
    inner = np.arange(1, CELLS + 1)
    x_side = axis_weights(np.concatenate([inner, [0, CELLS + 1]]), 0, PATCH_X)
    x_table = np.zeros((CELLS + 8, 16))
    x_table[: CELLS + 2, :PATCH_X] = x_side
    y_cells = np.arange(1 - EDGE, CELLS + EDGE + 1)
    y_side = axis_weights(y_cells, -1, PATCH_Y)
    y_out = axis_weights(np.array([-EDGE, CELLS + EDGE + 1]), -1, PATCH_Y)
    z_side = axis_weights(np.arange(CELLS + 2), 0, PATCH_Z)
    z_edge = np.zeros((CELLS, PATCH_Z))
    z_edge[0] = z_side[0]
    z_edge[-1] = z_side[-1]
    y_edge = np.zeros((LAYERS, PATCH_Y))
    y_edge[0] = y_out[0]
    y_edge[-1] = y_out[1]

    def both(ys, zs):
        return np.einsum("jb,kc->bcjk", ys, zs).reshape(PATCH_Y * PATCH_Z, WIDE)

    table = np.zeros((128, 3 * WIDE))
    table[: PATCH_Y * PATCH_Z] = np.concatenate(
        [both(y_side, z_side[1:-1]), both(y_side, z_edge), both(y_edge, z_side[1:-1])], axis=1
    )
    return x_table.astype(np.float32), table.astype(np.float32)


def from_behind(value, axis, steps):
    count = lax.axis_size(axis)
    initial, last = (max(0, -steps), min(count, count - steps))
    return lax.ppermute(value, axis, [(source, source + steps) for source in range(initial, last)])


def extended(block, axis, dim, width):
    count = lax.axis_size(axis)
    forward = [(i, (i + 1) % count) for i in range(count)]
    backward = [(target, source) for source, target in forward]
    low = lax.ppermute(
        lax.slice_in_dim(block, block.shape[dim] - width, None, axis=dim), axis, forward
    )
    high = lax.ppermute(lax.slice_in_dim(block, 0, width, axis=dim), axis, backward)
    return jnp.concatenate([low, block, high], axis=dim)


def decay(length, eig_first, eig_second):
    delta = -(eig_first + eig_second)
    delta = jnp.where(delta <= 0.0, 1.0, delta)
    q = 0.5 * delta + jnp.sqrt(delta + 0.25 * delta * delta)
    return 1.0 / (1.0 + q)


def moments_kernel(f_ref, eb_ref, ec_ref, out_ref):
    rows = f_ref.shape[0]
    r = decay(NR, eb_ref[...], ec_ref[...])
    up = f_ref[0]
    down = f_ref[rows - 1]
    for i in range(1, rows):
        up = r * up + f_ref[i]
        down = r * down + f_ref[rows - 1 - i]
    out_ref[0] = up
    out_ref[1] = down


def carry_kernel(rows, mom_ref, eb_ref, ec_ref, out_ref):
    blocks = mom_ref.shape[0]
    band = out_ref.shape[1] // 2
    r = decay(NR, eb_ref[...], ec_ref[...])
    ratio = r
    for _ in range(rows - 1):
        ratio = ratio * r
    total = jnp.ones_like(ratio)
    up = jnp.zeros_like(ratio)
    down = jnp.zeros_like(ratio)
    for k in range(blocks):
        total = total * ratio
        up = ratio * up + mom_ref[k, :band]
        down = ratio * down + mom_ref[blocks - 1 - k, band : 2 * band]
    norm = 1.0 / (1.0 - total)
    up = up * norm
    down = down * norm
    for k in range(blocks):
        out_ref[k, :band] = up
        up = ratio * up + mom_ref[k, :band]
        other = blocks - 1 - k
        out_ref[other, band : 2 * band] = down
        down = ratio * down + mom_ref[other, band : 2 * band]


def solve_kernel(f_ref, carry_ref, eb_ref, ec_ref, zero_ref, out_ref):
    rows = f_ref.shape[0]
    r = decay(NR, eb_ref[...], ec_ref[...])
    scale = -r / ((1.0 - r) * (1.0 + r))
    tile = f_ref.shape[1]
    first = lax.broadcasted_iota(jnp.int32, r.shape, 0) + pl.program_id(0) * tile
    second = lax.broadcasted_iota(jnp.int32, r.shape, 1)
    zero_mode = (first == 0) & (second == 0)
    up = carry_ref[0]
    for i in range(rows):
        up = r * up + f_ref[i]
        out_ref[i] = up
    down = carry_ref[1]
    for i in range(rows - 1, -1, -1):
        down = r * down
        value = (out_ref[i] + down) * scale
        out_ref[i] = jnp.where(zero_mode, zero_ref[i][None, :], value)
        down = down + f_ref[i]


def subgrid_kernel(
    flag_ref, patch_ref, xt_ref, yz_ref, mid_ref, low_ref, high_ref, vel_ref, pot_ref, kick_ref
):
    slot = pl.program_id(0)
    live = flag_ref[0, slot] > 0
    has_below = flag_ref[1, slot] > 0
    has_above = flag_ref[2, slot] > 0
    back_below = flag_ref[3, slot] > 0
    back_above = flag_ref[4, slot] > 0
    planes = jnp.dot(patch_ref[0], yz_ref[...], precision=HIGHEST, preferred_element_type=F32)
    coarse = jnp.dot(xt_ref[...], planes, precision=HIGHEST, preferred_element_type=F32)
    start = coarse[:CELLS, :WIDE]
    x_low = coarse[CELLS : CELLS + 1, :WIDE]
    x_high = coarse[CELLS + 1 : CELLS + 2, :WIDE]
    z_edge = coarse[:CELLS, WIDE : 2 * WIDE]
    y_edge = coarse[:CELLS, 2 * WIDE :]
    shape = (CELLS, WIDE)
    row = lax.broadcasted_iota(jnp.int32, shape, 0)
    lane = lax.broadcasted_iota(jnp.int32, shape, 1)
    third = lane % CELLS
    side = EDGE * CELLS
    end = WIDE - side
    y_above = jnp.where(lane >= WIDE - CELLS, y_edge, pltpu.roll(start, WIDE - CELLS, 1))
    y_below = jnp.where(lane < CELLS, y_edge, pltpu.roll(start, CELLS, 1))
    cut_above = (lane >= WIDE - CELLS) | (
        (lane >= side - CELLS) & (lane < side) & jnp.logical_not(back_below)
    )
    cut_below = (lane < CELLS) | (
        (lane >= end) & (lane < end + CELLS) & jnp.logical_not(back_above)
    )
    fixed = ((lane < side) & jnp.logical_not(has_below)) | (
        (lane >= end) & jnp.logical_not(has_above)
    )
    rho = jnp.concatenate([low_ref[0], mid_ref[0], high_ref[0]], axis=1) * (1.0 / (REF * REF))

    def beside(v):
        return (
            (
                jnp.where(row == 0, x_low, pltpu.roll(v, 1, 0)),
                jnp.where(row == CELLS - 1, x_high, pltpu.roll(v, CELLS - 1, 0)),
            ),
            (
                jnp.where(cut_below, y_below, pltpu.roll(v, CELLS, 1)),
                jnp.where(cut_above, y_above, pltpu.roll(v, WIDE - CELLS, 1)),
            ),
            (
                jnp.where(third == 0, z_edge, pltpu.roll(v, 1, 1)),
                jnp.where(third == CELLS - 1, z_edge, pltpu.roll(v, WIDE - 1, 1)),
            ),
        )

    v = start
    for _ in range(SWEEPS):
        first, second, last = beside(v)
        total = first[1] + first[0] + second[1] + second[0] + last[1] + last[0]
        new = (1.0 - RELAXATION) * v + RELAXATION * (total - rho) / 6.0
        v = jnp.where(fixed, v, new)
    pot_ref[0] = jnp.where(live, v[:, side:end], 0.0)
    for q, (below, above) in enumerate(beside(v)):
        slope = (above[:, side:end] - below[:, side:end]) * (REF / 2.0)
        kick_ref[q, 0] = jnp.where(live, vel_ref[q, 0] - slope, 0.0)


def poisson(root_density):
    size_second = lax.axis_size("py")
    devices = lax.axis_size("px") * size_second
    device = lax.axis_index("px") * size_second + lax.axis_index("py")
    basis = jnp.asarray(fourier_basis(NR), F32)
    eig = -4.0 * np.sin(np.pi / NR * np.arange(NR)) ** 2
    eig_first = jnp.asarray(eig[:, None], F32)
    eig_second = jnp.asarray(eig[None, :], F32)
    rows = NR // devices
    band = NR // devices
    planes = lax.all_to_all(root_density, "py", split_axis=0, concat_axis=1, tiled=True)
    f = jnp.einsum("xyz,cz->xyc", planes, basis, precision=HIGH)
    f = jnp.einsum("xyc,by->xbc", f, basis, precision=HIGH)
    tile = 48
    grid = NR // tile
    f_spec = pl.BlockSpec((rows, tile, NR), lambda t: (0, t, 0))
    pair_spec = pl.BlockSpec((2, tile, NR), lambda t: (0, t, 0))
    eb_spec = pl.BlockSpec((tile, 1), lambda t: (t, 0))
    ec_spec = pl.BlockSpec((1, NR), lambda t: (0, 0))
    params = pltpu.CompilerParams(
        dimension_semantics=("arbitrary",), vmem_limit_bytes=60 * 1024 * 1024
    )
    moments = pl.pallas_call(
        moments_kernel,
        grid=(grid,),
        in_specs=[f_spec, eb_spec, ec_spec],
        out_specs=pair_spec,
        out_shape=jax.ShapeDtypeStruct((2, NR, NR), F32),
        compiler_params=params,
    )(f, eig_first, eig_second)
    column = jnp.pad(f[:, 0, 0], (0, NR - rows))
    sent = jnp.concatenate(
        [
            moments.reshape(2, devices, band, NR).transpose(1, 0, 2, 3).reshape(
                devices, 2 * band, NR
            ),
            jnp.broadcast_to(column[None, None, :], (devices, 8, NR)),
        ],
        axis=1,
    )
    got = lax.all_to_all(sent, ("px", "py"), split_axis=0, concat_axis=0, tiled=True)
    carries = pl.pallas_call(
        lambda *refs: carry_kernel(rows, *refs),
        out_shape=jax.ShapeDtypeStruct((devices, 2 * band, NR), F32),
        compiler_params=pltpu.CompilerParams(vmem_limit_bytes=60 * 1024 * 1024),
    )(got, lax.dynamic_slice_in_dim(eig_first, device * band, band, 0), eig_second)
    back = lax.all_to_all(carries, ("px", "py"), split_axis=0, concat_axis=0, tiled=True)
    back = back.reshape(devices, 2, band, NR).transpose(1, 0, 2, 3).reshape(2, NR, NR)
    whole_column = got[:, 2 * band, :rows].reshape(NR)
    own = lax.dynamic_slice_in_dim(
        jnp.asarray(pseudo_inverse(NR), F32), device * rows, rows, 0
    )
    zero_values = jnp.sum(own * whole_column[None, :], axis=1)
    zero_wide = jnp.broadcast_to(zero_values[:, None], (rows, NR))
    u = pl.pallas_call(
        solve_kernel,
        grid=(grid,),
        in_specs=[f_spec, pair_spec, eb_spec, ec_spec, pl.BlockSpec((rows, NR), lambda t: (0, 0))],
        out_specs=f_spec,
        out_shape=jax.ShapeDtypeStruct((rows, NR, NR), F32),
        compiler_params=params,
    )(f, back, eig_first, eig_second, zero_wide)
    u = jnp.einsum("xbc,by->xyc", u, basis, precision=HIGH)
    u = jnp.einsum("xyc,cz->xyz", u, basis, precision=HIGH)
    return lax.all_to_all(u, "py", split_axis=1, concat_axis=0, tiled=True)


def local(root_density, subgrid_density, velocity, slot_anchor, slot_count, neighbour):
    first_rows, second_rows = root_density.shape[:2]
    size_second = lax.axis_size("py")
    place_first = lax.axis_index("px")
    place_second = lax.axis_index("py")
    device = place_first * size_second + place_second
    per_device = subgrid_density.shape[0]
    side = EDGE * CELLS
    inner = CELLS * CELLS
    low_density = from_behind(subgrid_density[:, :, inner - side :], "py", 1)
    high_density = from_behind(subgrid_density[:, :, :side], "py", -1)
    coarse_potential = poisson(root_density)
    padded = extended(extended(coarse_potential, "px", 0, 1), "py", 1, 2)
    patches = []
    for target in range(size_second):
        owner = place_first * size_second + target
        wanted = (place_second - target) % size_second
        anchor = slot_anchor[:, owner * per_device + wanted]
        x = jnp.clip(anchor[0] - place_first * first_rows, 0, first_rows - REG)
        y = jnp.clip(anchor[1] - place_second * second_rows, 0, second_rows - REG)
        cut = lax.dynamic_slice(padded, (x, y, 0), (PATCH_X, PATCH_Y, NR))
        columns = (anchor[2] - 1 + jnp.arange(PATCH_Z, dtype=jnp.int32)) % NR
        pick = (jnp.arange(NR, dtype=jnp.int32)[:, None] == columns[None, :]).astype(F32)
        patches.append(
            jnp.dot(cut.reshape(PATCH_X * PATCH_Y, NR), pick, precision=HIGHEST).reshape(-1)
        )
    arrived = lax.all_to_all(
        jnp.stack(patches), "py", split_axis=0, concat_axis=0, tiled=True
    )
    positions = jnp.arange(per_device, dtype=jnp.int32)
    patch = arrived[(place_second + positions) % size_second]
    patch = patch.reshape(per_device, PATCH_X, PATCH_Y * PATCH_Z)
    patch = jnp.pad(
        patch, ((0, 0), (0, 16 - PATCH_X), (0, 128 - PATCH_Y * PATCH_Z))
    )
    slots = device * per_device + positions
    below, above = neighbour[0][slots], neighbour[1][slots]
    flags = jnp.stack(
        [
            positions < slot_count[device],
            below >= 0,
            above >= 0,
            neighbour[1][jnp.maximum(below, 0)] >= 0,
            neighbour[0][jnp.maximum(above, 0)] >= 0,
        ]
    ).astype(jnp.int32)
    x_table, yz_table = patch_tables()
    slot_spec = lambda width: pl.BlockSpec((1, CELLS, width), lambda s: (s, 0, 0))
    vel_spec = pl.BlockSpec((3, 1, CELLS, inner), lambda s: (0, s, 0, 0))
    potential, kicked = pl.pallas_call(
        subgrid_kernel,
        grid=(per_device,),
        in_specs=[
            pl.BlockSpec(memory_space=pltpu.SMEM),
            pl.BlockSpec((1, 16, 128), lambda s: (s, 0, 0)),
            pl.BlockSpec(x_table.shape, lambda s: (0, 0)),
            pl.BlockSpec(yz_table.shape, lambda s: (0, 0)),
            slot_spec(inner),
            slot_spec(side),
            slot_spec(side),
            vel_spec,
        ],
        out_specs=[slot_spec(inner), vel_spec],
        out_shape=[
            jax.ShapeDtypeStruct(subgrid_density.shape, F32),
            jax.ShapeDtypeStruct(velocity.shape, F32),
        ],
        compiler_params=pltpu.CompilerParams(
            dimension_semantics=("arbitrary",), vmem_limit_bytes=60 * 1024 * 1024
        ),
    )(
        flags,
        patch,
        jnp.asarray(x_table),
        jnp.asarray(yz_table),
        subgrid_density,
        low_density,
        high_density,
        velocity,
    )
    return (coarse_potential, potential, kicked)


def solution(mesh):
    return jax.shard_map(
        local,
        mesh=mesh,
        in_specs=(
            P("px", "py", None),
            P(("px", "py"), None, None),
            P(None, ("px", "py"), None, None),
            P(),
            P(),
            P(),
        ),
        out_specs=(
            P("px", "py", None),
            P(("px", "py"), None, None),
            P(None, ("px", "py"), None, None),
        ),
        check_vma=False,
    )
```

time: 2300 us -> 596 us (0.26)
  the two profiles are of different devices: /device:TPU:5 before, /device:TPU:0 now
where the time goes in v1:
time: 596 us; the launch traced here: 586 us
  waiting for transfers between devices  264 us (44%)
  blocking collectives  162 us (27%)
  local copies, waits for them, and re-layouts  41.5 us (7%)
  Pallas kernels  38.3 us (6%)
  matrix products  31.4 us (5%)
  starting transfers between devices  26.8 us (4%)
  between operations  17.1 us (3%)
    all_to_all x1, waiting for transfers between devices, poisson(): return lax.all_to_all(u, 'py', split_axis=1, concat_axis=0, tiled=True)  176 us
    all_to_all x1, blocking collectives, poisson(): lax.all_to_all(root_density, 'py', split_axis=0, concat_axis=1, tiled=True)  162 us
    all_to_all x1, waiting for transfers between devices, poisson(): lax.all_to_all(sent, ('px', 'py'), split_axis=0, concat_axis=0, tiled=True)  37.5 us
    all_to_all x1, waiting for transfers between devices, poisson(): lax.all_to_all(carries, ('px', 'py'), split_axis=0, concat_axis=0, tiled=...  28.4 us
    pallas_call x1, Pallas kernels, local(): pl.pallas_call(subgrid_kernel, grid=(per_device,), in_specs=[pl.BlockSpec...  18.6 us
    ppermute x2, waiting for transfers between devices, extended(): lax.ppermute(lax.slice_in_dim(block, block.shape[dim] - width, None, axis...  12.9 us
  transfers between devices with their start and end apart: 10, of which 7 were waited for; matrix products, arithmetic and copies ran while one was open for 5% of the time, Pallas kernels for 0%

profile of v1, /device:TPU:0, one launch (start us, length us, event | category | flops | bytes accessed | tf_op | source)
XLA Modules:
  0.0 586.3 jit_solution(2053867442889195879)
XLA Ops:
  0.6 162.3 %all_to_all.58 = f32[96,48,384]{2,1,0:T(8,128)S(1)} all-to-all(f32[96,48,384]{2,1,0:T(8,128)} %param.12), channel_id=1, replica_groups=mesh['px'=4,'py'=8] {'py'}, dimensions={0} | all-to-all | bytes 14155776 | tf_op jit(solution)/shard_map/all_to_all | solution.py:242
  164.0 6.1 %fusion.37 = f32[384,12,384]{2,0,1:T(8,128)S(1)} fusion(f32[384,384,1]{1,0,2:T(8,128)S(1)} %copy-done.2, f32[12,384,384]{2,1,0:T(8,128)S(1)} %bitcast.92), kind=kOutput, calls=%fused_computation.98 | convolution fusion | flops 4076863488 | bytes 14745600 | tf_op jit(solution)/shard_map/xyz,cz->xyc/dot_general | solution.py:243
  170.1 5.9 %fusion.4.f_ref = f32[12,384,384]{2,1,0:T(8,128)S(1)} fusion(f32[384,384,1]{1,0,2:T(8,128)S(1)} %copy-done.2, f32[384,12,384]{2,0,1:T(8,128)S(1)} %fusion.37), kind=kOutput, calls=%fused_computation.10 | convolution fusion | flops 4076863488 | bytes 14745600 | tf_op jit(solution)/shard_map/xyc,by->xbc/dot_general | solution.py:244
  176.0 3.0 copy-done.1
  179.2 7.4 %shard_map.139 = f32[2,384,384]{2,1,0:T(8,128)} custom-call(f32[12,384,384]{2,1,0:T(8,128)} %copy-done.1, f32[384,1]{1,0:T(8,128)} %constant.189.clone.eb_ref, f32[1,384]{1,0:T(1,128)} %constant.190.clone.ec_ref.refs_2_), custom_call_target="tpu_custom_call" | custom-call | tf_op jit(solution)/shard_map/pallas_call | solution.py:254
  186.5 2.2 copy.128
  189.7 1.3 pad_maximum_fusion.1
  191.0 3.6 all-to-all-start.1
  194.6 1.3 constant_dynamic-slice_fusion.16.refs_1_
  195.9 37.5 %all-to-all-done.1.refs_0_ = f32[32,32,384]{2,1,0:T(8,128)S(1)} async-done(((f32[32,32,384]{2,1,0:T(8,128)}), f32[32,32,384]{2,1,0:T(8,128)S(1)}, u32[]{:S(2)}, u32[]{:S(2)}) %all-to-all-start.1) | async-done | bytes 1572896 | tf_op jit(solution)/shard_map/all_to_all | solution.py:272
  234.6 2.9 shard_map.140
  237.4 2.7 all-to-all-start.2
  242.1 28.4 %all-to-all-done.2 = f32[32,24,384]{2,1,0:T(8,128)S(1)} async-done(((f32[32,24,384]{2,1,0:T(8,128)}), f32[32,24,384]{2,1,0:T(8,128)S(1)}, u32[]{:S(2)}, u32[]{:S(2)}) %all-to-all-start.2) | async-done | bytes 1179680 | tf_op jit(solution)/shard_map/all_to_all | solution.py:278
  273.3 9.4 %shard_map.141 = f32[12,384,384]{2,1,0:T(8,128)} custom-call(f32[12,384,384]{2,1,0:T(8,128)} %copy-done.1, f32[2,384,384]{2,1,0:T(8,128)} %copy.133.carry_ref, f32[384,1]{1,0:T(8,128)} %constant.189.clone.eb_ref, f32[1,384]{1,0:T(1,128)} %constant.190.clone.ec_ref.refs_2_, f32[12,384]{1,0:T(8,128)} %broadcast_in_dim.5.zero_ref), custom_call_target="tpu_custom_call" | custom-call | tf_op jit(solution)/shard_map/pallas_call | solution.py:286
  282.7 9.4 %fusion.38 = f32[12,384,384]{2,1,0:T(8,128)S(1)} fusion(f32[12,384,384]{2,1,0:T(8,128)} %shard_map.141, f32[384,384,1]{1,0,2:T(8,128)S(1)} %copy-done.2), kind=kOutput, calls=%fused_computation.99 | convolution fusion | flops 4076863488 | bytes 14745600 | tf_op jit(solution)/shard_map/xbc,by->xyc/dot_general | solution.py:294
  292.2 7.8 %fusion = f32[12,384,384]{2,1,0:T(8,128)S(1)} fusion(f32[384,384,1]{1,0,2:T(8,128)S(1)} %copy-done.2, f32[12,384,384]{2,1,0:T(8,128)S(1)} %fusion.38), kind=kOutput, calls=%fused_computation.6 | convolution fusion | flops 4076863488 | bytes 14745600 | tf_op jit(solution)/shard_map/xyc,cz->xyz/dot_general | solution.py:295
  299.9 7.8 %copy.136 = f32[12,384,384]{2,0,1:T(8,128)} copy(f32[12,384,384]{2,1,0:T(8,128)S(1)} %fusion) | data formatting | bytes 14155776 | tf_op jit(solution)/shard_map/xyc,cz->xyz/dot_general | solution.py:295
  307.8 5.2 all-to-all-start.3
  314.0 3.8 collective-permute-start.4
  317.8 1.5 collective-permute-start.5
  344.2 175.7 %all-to-all-done.3 = f32[12,384,384]{2,0,1:T(8,128)} async-done(((f32[12,384,384]{2,0,1:T(8,128)}), f32[12,384,384]{2,0,1:T(8,128)}, u32[]{:S(2)}, u32[]{:S(2)}) %all-to-all-start.3) | async-done | bytes 7077920 | tf_op jit(solution)/shard_map/all_to_all | solution.py:296
  519.9 5.8 copy.138
  525.8 1.7 collective-permute-start.1
  527.5 2.0 collective-permute-done
  529.8 1.7 collective-permute-start.2
  531.5 3.1 collective-permute-start.3
  534.7 10.8 %collective-permute-done.2 = f32[98,2,384]{2,0,1:T(8,128)S(1)} collective-permute-done((f32[98,2,384]{2,0,1:T(8,128)S(1)}, f32[98,2,384]{2,0,1:T(8,128)S(1)}, u32[]{:S(2)}, u32[]{:S(2)}) %collective-permute-start.2) | collective-permute-done | bytes 301088 | tf_op jit(solution)/shard_map/ppermute | solution.py:98
  545.7 2.7 collective-permute-done.3
  548.5 1.4 pad_maximum_fusion
  554.6 3.3 all-to-all-start.4
  558.0 6.7 %all-to-all-done.4 = f32[8,1,1200]{2,1,0:T(1,128)S(1)} async-done(((f32[8,1,1200]{2,1,0:T(1,128)}), f32[8,1,1200]{2,1,0:T(1,128)S(1)}, u32[]{:S(2)}, u32[]{:S(2)}) %all-to-all-start.4) | async-done | bytes 38432 | tf_op jit(solution)/shard_map/all_to_all | solution.py:325
  567.2 18.6 %shard_map.142 = (f32[8,32,1024]{2,1,0:T(8,128)}, f32[3,8,32,1024]{3,2,1,0:T(8,128)}) custom-call(s32[5,8]{1,0:T(8,128)} %convert_element_type.5.flag_ref, f32[8,16,128]{2,1,0:T(8,128)} %pad.9.patch_ref, f32[40,16]{1,0:T(8,128)} %constant.192.clone.xt_ref, f32[128,3840]{1,0:T(8,128)} %constant.193.clone.yz_ref, f32[8,32,1024]{2,1,0:T(8,128)} %mid_ref.1, ...), custom_call_target="tpu_custom_call" | custom-call | tf_op jit(solution)/shard_map/pallas_call | solution.py:348
  (104 shorter events, 26.2 us)
Async XLA Ops:
  162.9 1.1 copy-start.2
  176.0 3.0 copy-start.1
  191.0 42.4 %all-to-all-start.1 = ((f32[32,32,384]{2,1,0:T(8,128)}), f32[32,32,384]{2,1,0:T(8,128)S(1)}, u32[]{:S(2)}, u32[]{:S(2)}) async-start(f32[32,32,384]{2,1,0:T(8,128)} %pad_maximum_fusion.1), calls=%async_computation.1 | async-start | bytes 3145728 | tf_op jit(solution)/shard_map/all_to_all | solution.py:272
  233.4 1.1 copy-start.3
  237.4 33.0 %all-to-all-start.2 = ((f32[32,24,384]{2,1,0:T(8,128)}), f32[32,24,384]{2,1,0:T(8,128)S(1)}, u32[]{:S(2)}, u32[]{:S(2)}) async-start(f32[32,24,384]{2,1,0:T(8,128)} %shard_map.140), calls=%async_computation.2 | async-start | bytes 2359296 | tf_op jit(solution)/shard_map/all_to_all | solution.py:278
  307.8 11.7 %copy-start.6 = (s32[3,256]{1,0:T(4,128)S(1)}, s32[3,256]{1,0:T(4,128)}, u32[]{:S(2)}) copy-start(s32[3,256]{1,0:T(4,128)} %param.15) | copy-start | bytes 9220
  307.8 31.8 %copy-start.7 = (s32[2,256]{1,0:T(2,128)S(1)}, s32[2,256]{1,0:T(2,128)}, u32[]{:S(2)}) copy-start(s32[2,256]{1,0:T(2,128)} %param.17) | copy-start | bytes 6148
  307.8 34.5 %copy-start.8 = (s32[32]{0:T(128)S(1)}, s32[32]{0:T(128)}, u32[]{:S(2)}) copy-start(s32[32]{0:T(128)} %param.16) | copy-start | bytes 388
  307.8 212.1 %all-to-all-start.3 = ((f32[12,384,384]{2,0,1:T(8,128)}), f32[12,384,384]{2,0,1:T(8,128)}, u32[]{:S(2)}, u32[]{:S(2)}) async-start(f32[12,384,384]{2,0,1:T(8,128)} %copy.136), calls=%async_computation.3 | async-start | bytes 18874368 | tf_op jit(solution)/shard_map/all_to_all | solution.py:296
  314.0 252.0 %collective-permute-start.4 = (f32[8,32,128]{2,1,0:T(8,128)S(1)}, f32[8,32,128]{2,1,0:T(8,128)S(1)}, u32[]{:S(2)}, u32[]{:S(2)}) collective-permute-start(f32[8,32,128]{2,1,0:T(8,128)S(1)} %get-tuple-element.23), channel_id=1, source_target_pairs={{0,1},{1,2},{2,3},{3,4},{4,5},{5,6},{6,7},{8,9},{9,10},{10,11},{11... | collective-permute-start | bytes 393224 | tf_op jit(solution)/shard_map/ppermute | solution.py:91
  317.8 248.2 %collective-permute-start.5 = (f32[8,32,128]{2,1,0:T(8,128)S(1)}, f32[8,32,128]{2,1,0:T(8,128)S(1)}, u32[]{:S(2)}, u32[]{:S(2)}) collective-permute-start(f32[8,32,128]{2,1,0:T(8,128)S(1)} %get-tuple-element.22), channel_id=1, source_target_pairs={{1,0},{2,1},{3,2},{4,3},{5,4},{6,5},{7,6},{9,8},{10,9},{11,10},{12... | collective-permute-start | bytes 393224 | tf_op jit(solution)/shard_map/ppermute | solution.py:91
  525.7 24.3 %copy-start = (f32[8,12,48,384]{3,2,1,0:T(8,128)}, f32[8,12,48,384]{3,2,1,0:T(8,128)S(1)}, u32[]{:S(2)}) copy-start(f32[8,12,48,384]{3,2,1,0:T(8,128)S(1)} %copy.138) | copy-start | bytes 21233668
  525.7 3.8 collective-permute-start
  525.8 3.8 collective-permute-start.1
  529.8 15.7 %collective-permute-start.2 = (f32[98,2,384]{2,0,1:T(8,128)S(1)}, f32[98,2,384]{2,0,1:T(8,128)S(1)}, u32[]{:S(2)}, u32[]{:S(2)}) collective-permute-start(f32[98,2,384]{2,0,1:T(8,128)S(1)} %copy.139), channel_id=1, source_target_pairs={{0,1},{1,2},{2,3},{3,4},{4,5},{5,6},{6,7},{7,0},{8,9},{9,10},{10,1... | collective-permute-start | bytes 903176 | tf_op jit(solution)/shard_map/ppermute | solution.py:98
  531.5 16.9 %collective-permute-start.3 = (f32[98,2,384]{2,0,1:T(8,128)S(1)}, f32[98,2,384]{2,0,1:T(8,128)S(1)}, u32[]{:S(2)}, u32[]{:S(2)}) collective-permute-start(f32[98,2,384]{2,0,1:T(8,128)S(1)} %copy.140), channel_id=1, source_target_pairs={{1,0},{2,1},{3,2},{4,3},{5,4},{6,5},{7,6},{0,7},{9,8},{10,9},{11,1... | collective-permute-start | bytes 903176 | tf_op jit(solution)/shard_map/ppermute | solution.py:101
  554.6 10.0 %all-to-all-start.4 = ((f32[8,1,1200]{2,1,0:T(1,128)}), f32[8,1,1200]{2,1,0:T(1,128)S(1)}, u32[]{:S(2)}, u32[]{:S(2)}) async-start(f32[8,1,1200]{2,1,0:T(1,128)} %copy.151), calls=%async_computation.4 | async-start | bytes 81920 | tf_op jit(solution)/shard_map/all_to_all | solution.py:325
  566.0 0.6 copy-start.4
  566.6 0.6 copy-start.5

commit v2 on v1

--- a/solution.py
+++ b/solution.py
@@ -121,7 +121,7 @@
     out_ref[1] = down
 
 
-def carry_kernel(rows, mom_ref, eb_ref, ec_ref, out_ref):
+def carry_kernel(rows, order, mom_ref, eb_ref, ec_ref, out_ref):
     blocks = mom_ref.shape[0]
     band = out_ref.shape[1] // 2
     r = decay(NR, eb_ref[...], ec_ref[...])
@@ -133,15 +133,15 @@
     down = jnp.zeros_like(ratio)
     for k in range(blocks):
         total = total * ratio
-        up = ratio * up + mom_ref[k, :band]
-        down = ratio * down + mom_ref[blocks - 1 - k, band : 2 * band]
+        up = ratio * up + mom_ref[order[k], :band]
+        down = ratio * down + mom_ref[order[blocks - 1 - k], band : 2 * band]
     norm = 1.0 / (1.0 - total)
     up = up * norm
     down = down * norm
     for k in range(blocks):
-        out_ref[k, :band] = up
-        up = ratio * up + mom_ref[k, :band]
-        other = blocks - 1 - k
+        out_ref[order[k], :band] = up
+        up = ratio * up + mom_ref[order[k], :band]
+        other = order[blocks - 1 - k]
         out_ref[other, band : 2 * band] = down
         down = ratio * down + mom_ref[other, band : 2 * band]
 
@@ -230,18 +230,23 @@
 
 
 def poisson(root_density):
+    size_first = lax.axis_size("px")
     size_second = lax.axis_size("py")
-    devices = lax.axis_size("px") * size_second
+    devices = size_first * size_second
     device = lax.axis_index("px") * size_second + lax.axis_index("py")
+    block = lax.axis_index("py") * size_first + lax.axis_index("px")
+    order = [(k % size_first) * size_second + k // size_first for k in range(devices)]
     basis = jnp.asarray(fourier_basis(NR), F32)
     eig = -4.0 * np.sin(np.pi / NR * np.arange(NR)) ** 2
     eig_first = jnp.asarray(eig[:, None], F32)
     eig_second = jnp.asarray(eig[None, :], F32)
     rows = NR // devices
     band = NR // devices
-    planes = lax.all_to_all(root_density, "py", split_axis=0, concat_axis=1, tiled=True)
-    f = jnp.einsum("xyz,cz->xyc", planes, basis, precision=HIGH)
-    f = jnp.einsum("xyc,by->xbc", f, basis, precision=HIGH)
+    planes = lax.all_to_all(
+        jnp.transpose(root_density, (1, 0, 2)), "px", split_axis=0, concat_axis=1, tiled=True
+    )
+    f = jnp.einsum("yxz,cz->yxc", planes, basis, precision=HIGH)
+    f = jnp.einsum("yxc,ax->yac", f, basis, precision=HIGH)
     tile = 48
     grid = NR // tile
     f_spec = pl.BlockSpec((rows, tile, NR), lambda t: (0, t, 0))
@@ -271,15 +276,16 @@
     )
     got = lax.all_to_all(sent, ("px", "py"), split_axis=0, concat_axis=0, tiled=True)
     carries = pl.pallas_call(
-        lambda *refs: carry_kernel(rows, *refs),
+        lambda *refs: carry_kernel(rows, order, *refs),
         out_shape=jax.ShapeDtypeStruct((devices, 2 * band, NR), F32),
         compiler_params=pltpu.CompilerParams(vmem_limit_bytes=60 * 1024 * 1024),
     )(got, lax.dynamic_slice_in_dim(eig_first, device * band, band, 0), eig_second)
     back = lax.all_to_all(carries, ("px", "py"), split_axis=0, concat_axis=0, tiled=True)
     back = back.reshape(devices, 2, band, NR).transpose(1, 0, 2, 3).reshape(2, NR, NR)
-    whole_column = got[:, 2 * band, :rows].reshape(NR)
+    whole_column = got[:, 2 * band, :rows].reshape(size_first, size_second, rows)
+    whole_column = whole_column.transpose(1, 0, 2).reshape(NR)
     own = lax.dynamic_slice_in_dim(
-        jnp.asarray(pseudo_inverse(NR), F32), device * rows, rows, 0
+        jnp.asarray(pseudo_inverse(NR), F32), block * rows, rows, 0
     )
     zero_values = jnp.sum(own * whole_column[None, :], axis=1)
     zero_wide = jnp.broadcast_to(zero_values[:, None], (rows, NR))
@@ -291,9 +297,10 @@
         out_shape=jax.ShapeDtypeStruct((rows, NR, NR), F32),
         compiler_params=params,
     )(f, back, eig_first, eig_second, zero_wide)
-    u = jnp.einsum("xbc,by->xyc", u, basis, precision=HIGH)
-    u = jnp.einsum("xyc,cz->xyz", u, basis, precision=HIGH)
-    return lax.all_to_all(u, "py", split_axis=1, concat_axis=0, tiled=True)
+    u = jnp.einsum("yac,ax->yxc", u, basis, precision=HIGH)
+    u = jnp.einsum("yxc,cz->yxz", u, basis, precision=HIGH)
+    u = lax.all_to_all(u, "px", split_axis=1, concat_axis=0, tiled=True)
+    return jnp.transpose(u, (1, 0, 2))
 
 
 def local(root_density, subgrid_density, velocity, slot_anchor, slot_count, neighbour):

time: 596 us -> 419 us (0.70)
  waiting for transfers between devices: 264 us -> 155 us
  blocking collectives: 162 us -> 83.1 us
  local copies, waits for them, and re-layouts: 41.5 us -> 57.1 us
    all_to_all x1, waiting for transfers between devices: 176 us -> 74.8 us  [poisson(): u = lax.all_to_all(u, 'px', split_axis=1, concat_axis=0, tiled=True)]
    all_to_all x1, blocking collectives: 162 us -> 83.1 us  [poisson(): lax.all_to_all(jnp.transpose(root_density, (1, 0, 2)), 'px', split_axis=0...]
    unnamed x19 -> x21, local copies, waits for them, and re-layouts: 5.73 us -> 21.2 us
    all_to_all x1, waiting for transfers between devices: 6.66 us -> 0.01 us  [local(): lax.all_to_all(jnp.stack(patches), 'py', split_axis=0, concat_axis=0, til...]
  transfers between devices with their start and end apart: 10 -> 10, of which waited for: 7 -> 6; matrix products, arithmetic and copies ran while one was open for 5% -> 9% of each run, Pallas kernels for 0% -> 0%
where the time goes in v2:
time: 419 us; the launch traced here: 415 us
  waiting for transfers between devices  155 us (37%)
  blocking collectives  83.1 us (20%)
  local copies, waits for them, and re-layouts  57.1 us (14%)
  Pallas kernels  38.3 us (9%)
  matrix products  31.9 us (8%)
  starting transfers between devices  27.8 us (7%)
  between operations  16.7 us (4%)
  other arithmetic  4.72 us (1%)
    all_to_all x1, blocking collectives, poisson(): lax.all_to_all(jnp.transpose(root_density, (1, 0, 2)), 'px', split_axis=0...  83.1 us
    all_to_all x1, waiting for transfers between devices, poisson(): u = lax.all_to_all(u, 'px', split_axis=1, concat_axis=0, tiled=True)  74.8 us
    all_to_all x1, waiting for transfers between devices, poisson(): lax.all_to_all(sent, ('px', 'py'), split_axis=0, concat_axis=0, tiled=True)  37.5 us
    all_to_all x1, waiting for transfers between devices, poisson(): lax.all_to_all(carries, ('px', 'py'), split_axis=0, concat_axis=0, tiled=...  28.4 us
    unnamed x21, local copies, waits for them, and re-layouts  21.2 us
    pallas_call x1, Pallas kernels, local(): pl.pallas_call(subgrid_kernel, grid=(per_device,), in_specs=[pl.BlockSpec...  18.6 us
    ppermute x2, waiting for transfers between devices, extended(): lax.ppermute(lax.slice_in_dim(block, block.shape[dim] - width, None, axis...  12.3 us
    dot_general x1, matrix products, poisson(): u = jnp.einsum('yac,ax->yxc', u, basis, precision=HIGH)  9.72 us
  transfers between devices with their start and end apart: 10, of which 6 were waited for; matrix products, arithmetic and copies ran while one was open for 9% of the time, Pallas kernels for 0%

profile of v2, /device:TPU:0, one launch (start us, length us, event | category | flops | bytes accessed | tf_op | source)
XLA Modules:
  0.0 414.9 jit_solution(150971887173553123)
XLA Ops:
  0.6 5.3 %copy.182 = f32[96,48,384]{2,0,1:T(8,128)S(1)} copy(f32[96,48,384]{2,1,0:T(8,128)} %param.12) | data formatting | bytes 14155776 | tf_op args[0]
  5.9 83.1 %all_to_all.58 = f32[48,96,384]{2,1,0:T(8,128)S(1)} all-to-all(f32[48,96,384]{2,1,0:T(8,128)S(1)} %bitcast.103), channel_id=1, replica_groups=mesh['px'=4,'py'=8] {'px'}, dimensions={0} | all-to-all | bytes 14155776 | tf_op jit(solution)/shard_map/all_to_all | solution.py:245
  90.1 6.1 %fusion.37 = f32[384,12,384]{2,0,1:T(8,128)S(1)} fusion(f32[384,384,1]{1,0,2:T(8,128)S(1)} %copy-done.2, f32[12,384,384]{2,1,0:T(8,128)S(1)} %bitcast.101), kind=kOutput, calls=%fused_computation.99 | convolution fusion | flops 4076863488 | bytes 14745600 | tf_op jit(solution)/shard_map/yxz,cz->yxc/dot_general | solution.py:248
  96.2 6.0 %fusion.4.f_ref = f32[12,384,384]{2,1,0:T(8,128)S(1)} fusion(f32[384,384,1]{1,0,2:T(8,128)S(1)} %copy-done.2, f32[384,12,384]{2,0,1:T(8,128)S(1)} %fusion.37), kind=kOutput, calls=%fused_computation.11 | convolution fusion | flops 4076863488 | bytes 14745600 | tf_op jit(solution)/shard_map/yxc,ax->yac/dot_general | solution.py:249
  102.2 3.0 copy-done.1
  105.4 7.4 %shard_map.139 = f32[2,384,384]{2,1,0:T(8,128)} custom-call(f32[12,384,384]{2,1,0:T(8,128)} %copy-done.1, f32[384,1]{1,0:T(8,128)} %constant.189.clone.eb_ref, f32[1,384]{1,0:T(1,128)} %constant.190.clone.ec_ref.refs_2_), custom_call_target="tpu_custom_call" | custom-call | tf_op jit(solution)/shard_map/pallas_call | solution.py:259
  112.7 2.2 copy.136
  115.9 1.3 pad_maximum_fusion.1
  117.2 5.1 %all-to-all-start.1 = ((f32[32,32,384]{2,1,0:T(8,128)}), f32[32,32,384]{2,1,0:T(8,128)S(1)}, u32[]{:S(2)}, u32[]{:S(2)}) async-start(f32[32,32,384]{2,1,0:T(8,128)} %pad_maximum_fusion.1), calls=%async_computation.1 | async-start | bytes 3145728 | tf_op jit(solution)/shard_map/all_to_all | solution.py:277
  122.3 1.3 constant_dynamic-slice_fusion.16.refs_1_
  123.6 37.5 %all-to-all-done.1.refs_0_ = f32[32,32,384]{2,1,0:T(8,128)S(1)} async-done(((f32[32,32,384]{2,1,0:T(8,128)}), f32[32,32,384]{2,1,0:T(8,128)S(1)}, u32[]{:S(2)}, u32[]{:S(2)}) %all-to-all-start.1) | async-done | bytes 1572896 | tf_op jit(solution)/shard_map/all_to_all | solution.py:277
  161.0 1.1 copy-done.3
  162.2 2.9 shard_map.140
  165.1 2.7 all-to-all-start.2
  169.7 28.4 %all-to-all-done.2 = f32[32,24,384]{2,1,0:T(8,128)S(1)} async-done(((f32[32,24,384]{2,1,0:T(8,128)}), f32[32,24,384]{2,1,0:T(8,128)S(1)}, u32[]{:S(2)}, u32[]{:S(2)}) %all-to-all-start.2) | async-done | bytes 1179680 | tf_op jit(solution)/shard_map/all_to_all | solution.py:283
  201.0 9.4 %shard_map.141 = f32[12,384,384]{2,1,0:T(8,128)} custom-call(f32[12,384,384]{2,1,0:T(8,128)} %copy-done.1, f32[2,384,384]{2,1,0:T(8,128)} %copy.142.carry_ref, f32[384,1]{1,0:T(8,128)} %constant.189.clone.eb_ref, f32[1,384]{1,0:T(1,128)} %constant.190.clone.ec_ref.refs_2_, f32[12,384]{1,0:T(8,128)} %broadcast_in_dim.5.zero_ref), custom_call_target="tpu_custom_call" | custom-call | tf_op jit(solution)/shard_map/pallas_call | solution.py:292
  210.4 9.7 %fusion.38 = f32[12,384,384]{2,1,0:T(8,128)S(1)} fusion(f32[12,384,384]{2,1,0:T(8,128)} %shard_map.141, f32[384,384,1]{1,0,2:T(8,128)S(1)} %copy-done.2), kind=kOutput, calls=%fused_computation.100 | convolution fusion | flops 4076863488 | bytes 14745600 | tf_op jit(solution)/shard_map/yac,ax->yxc/dot_general | solution.py:300
  220.1 7.8 %fusion = f32[12,384,384]{2,1,0:T(8,128)S(1)} fusion(f32[384,384,1]{1,0,2:T(8,128)S(1)} %copy-done.2, f32[12,384,384]{2,1,0:T(8,128)S(1)} %fusion.38), kind=kOutput, calls=%fused_computation.6 | convolution fusion | flops 4076863488 | bytes 14745600 | tf_op jit(solution)/shard_map/yxc,cz->yxz/dot_general | solution.py:301
  227.9 7.8 %copy.145 = f32[12,384,384]{2,0,1:T(8,128)} copy(f32[12,384,384]{2,1,0:T(8,128)S(1)} %fusion) | data formatting | bytes 14155776 | tf_op jit(solution)/shard_map/yxc,cz->yxz/dot_general | solution.py:301
  235.7 5.9 %all-to-all-start.3 = ((f32[12,384,384]{2,0,1:T(8,128)}), f32[12,384,384]{2,0,1:T(8,128)}, u32[]{:S(2)}, u32[]{:S(2)}) async-start(f32[12,384,384]{2,0,1:T(8,128)} %copy.145), calls=%async_computation.3 | async-start | bytes 18874368 | tf_op jit(solution)/shard_map/all_to_all | solution.py:302
  242.7 2.8 collective-permute-start.4
  245.5 1.3 collective-permute-start.5
  271.3 74.8 %all-to-all-done.3 = f32[12,384,384]{2,0,1:T(8,128)} async-done(((f32[12,384,384]{2,0,1:T(8,128)}), f32[12,384,384]{2,0,1:T(8,128)}, u32[]{:S(2)}, u32[]{:S(2)}) %all-to-all-start.3) | async-done | bytes 7077920 | tf_op jit(solution)/shard_map/all_to_all | solution.py:302
  346.1 5.8 %copy.147 = f32[4,12,96,384]{3,2,1,0:T(8,128)S(1)} copy(f32[4,12,96,384]{3,1,2,0:T(8,128)} %bitcast.18) | data formatting | bytes 14155776 | tf_op jit(solution)/shard_map/all_to_all | solution.py:302
  352.1 1.7 collective-permute-start.1
  353.9 2.1 collective-permute-done
  356.8 4.0 collective-permute-start.3
  360.9 10.2 %collective-permute-done.2 = f32[98,2,384]{2,0,1:T(8,128)S(1)} collective-permute-done((f32[98,2,384]{2,0,1:T(8,128)S(1)}, f32[98,2,384]{2,0,1:T(8,128)S(1)}, u32[]{:S(2)}, u32[]{:S(2)}) %collective-permute-start.2) | collective-permute-done | bytes 301088 | tf_op jit(solution)/shard_map/ppermute | solution.py:98
  371.1 2.2 collective-permute-done.3
  379.7 3.6 all-to-all-start.4
  383.3 10.1 %copy.165 = f32[96,48,384]{2,1,0:T(8,128)} copy(f32[96,48,384]{2,0,1:T(8,128)} %bitcast.100) | data formatting | bytes 14155776
  396.0 18.6 %shard_map.142 = (f32[8,32,1024]{2,1,0:T(8,128)}, f32[3,8,32,1024]{3,2,1,0:T(8,128)}) custom-call(s32[5,8]{1,0:T(8,128)} %convert_element_type.5.flag_ref, f32[8,16,128]{2,1,0:T(8,128)} %pad.9.patch_ref, f32[40,16]{1,0:T(8,128)} %constant.192.clone.xt_ref, f32[128,3840]{1,0:T(8,128)} %constant.193.clone.yz_ref, f32[8,32,1024]{2,1,0:T(8,128)} %mid_ref.1, ...), custom_call_target="tpu_custom_call" | custom-call | tf_op jit(solution)/shard_map/pallas_call | solution.py:355
  (111 shorter events, 27.0 us)
Async XLA Ops:
  89.0 1.1 copy-start.2
  102.2 3.0 copy-start.1
  117.2 43.9 %all-to-all-start.1 = ((f32[32,32,384]{2,1,0:T(8,128)}), f32[32,32,384]{2,1,0:T(8,128)S(1)}, u32[]{:S(2)}, u32[]{:S(2)}) async-start(f32[32,32,384]{2,1,0:T(8,128)} %pad_maximum_fusion.1), calls=%async_computation.1 | async-start | bytes 3145728 | tf_op jit(solution)/shard_map/all_to_all | solution.py:277
  161.0 1.1 copy-start.3
  165.1 33.0 %all-to-all-start.2 = ((f32[32,24,384]{2,1,0:T(8,128)}), f32[32,24,384]{2,1,0:T(8,128)S(1)}, u32[]{:S(2)}, u32[]{:S(2)}) async-start(f32[32,24,384]{2,1,0:T(8,128)} %shard_map.140), calls=%async_computation.2 | async-start | bytes 2359296 | tf_op jit(solution)/shard_map/all_to_all | solution.py:283
  235.7 11.2 %copy-start.6 = (s32[3,256]{1,0:T(4,128)S(1)}, s32[3,256]{1,0:T(4,128)}, u32[]{:S(2)}) copy-start(s32[3,256]{1,0:T(4,128)} %param.15) | copy-start | bytes 9220
  235.7 30.9 %copy-start.7 = (s32[2,256]{1,0:T(2,128)S(1)}, s32[2,256]{1,0:T(2,128)}, u32[]{:S(2)}) copy-start(s32[2,256]{1,0:T(2,128)} %param.17) | copy-start | bytes 6148
  235.7 33.6 %copy-start.8 = (s32[32]{0:T(128)S(1)}, s32[32]{0:T(128)}, u32[]{:S(2)}) copy-start(s32[32]{0:T(128)} %param.16) | copy-start | bytes 388
  235.7 110.3 %all-to-all-start.3 = ((f32[12,384,384]{2,0,1:T(8,128)}), f32[12,384,384]{2,0,1:T(8,128)}, u32[]{:S(2)}, u32[]{:S(2)}) async-start(f32[12,384,384]{2,0,1:T(8,128)} %copy.145), calls=%async_computation.3 | async-start | bytes 18874368 | tf_op jit(solution)/shard_map/all_to_all | solution.py:302
  242.7 152.0 %collective-permute-start.4 = (f32[8,32,128]{2,1,0:T(8,128)S(1)}, f32[8,32,128]{2,1,0:T(8,128)S(1)}, u32[]{:S(2)}, u32[]{:S(2)}) collective-permute-start(f32[8,32,128]{2,1,0:T(8,128)S(1)} %get-tuple-element.35), channel_id=1, source_target_pairs={{0,1},{1,2},{2,3},{3,4},{4,5},{5,6},{6,7},{8,9},{9,10},{10,11},{11... | collective-permute-start | bytes 393224 | tf_op jit(solution)/shard_map/ppermute | solution.py:91
  245.5 149.2 %collective-permute-start.5 = (f32[8,32,128]{2,1,0:T(8,128)S(1)}, f32[8,32,128]{2,1,0:T(8,128)S(1)}, u32[]{:S(2)}, u32[]{:S(2)}) collective-permute-start(f32[8,32,128]{2,1,0:T(8,128)S(1)} %get-tuple-element.34), channel_id=1, source_target_pairs={{1,0},{2,1},{3,2},{4,3},{5,4},{6,5},{7,6},{9,8},{10,9},{11,10},{12... | collective-permute-start | bytes 393224 | tf_op jit(solution)/shard_map/ppermute | solution.py:91
  351.9 22.4 %copy-start = (f32[4,12,96,384]{3,2,1,0:T(8,128)}, f32[4,12,96,384]{3,2,1,0:T(8,128)S(1)}, u32[]{:S(2)}) copy-start(f32[4,12,96,384]{3,2,1,0:T(8,128)S(1)} %copy.147) | copy-start | bytes 21233668
  352.0 3.9 collective-permute-start
  352.1 3.9 collective-permute-start.1
  356.0 15.0 %collective-permute-start.2 = (f32[98,2,384]{2,0,1:T(8,128)S(1)}, f32[98,2,384]{2,0,1:T(8,128)S(1)}, u32[]{:S(2)}, u32[]{:S(2)}) collective-permute-start(f32[98,2,384]{2,0,1:T(8,128)S(1)} %get-tuple-element.30), channel_id=1, source_target_pairs={{0,1},{1,2},{2,3},{3,4},{4,5},{5,6},{6,7},{7,0},{8,9},{9,10},{10,1... | collective-permute-start | bytes 903176 | tf_op jit(solution)/shard_map/ppermute | solution.py:98
  356.8 16.5 %collective-permute-start.3 = (f32[98,2,384]{2,0,1:T(8,128)S(1)}, f32[98,2,384]{2,0,1:T(8,128)S(1)}, u32[]{:S(2)}, u32[]{:S(2)}) collective-permute-start(f32[98,2,384]{2,0,1:T(8,128)S(1)} %get-tuple-element.31), channel_id=1, source_target_pairs={{1,0},{2,1},{3,2},{4,3},{5,4},{6,5},{7,6},{0,7},{9,8},{10,9},{11,1... | collective-permute-start | bytes 903176 | tf_op jit(solution)/shard_map/ppermute | solution.py:101
  379.7 13.6 %all-to-all-start.4 = ((f32[8,1,1200]{2,1,0:T(1,128)}), f32[8,1,1200]{2,1,0:T(1,128)S(1)}, u32[]{:S(2)}, u32[]{:S(2)}) async-start(f32[8,1,1200]{2,1,0:T(1,128)} %copy.164), calls=%async_computation.4 | async-start | bytes 81920 | tf_op jit(solution)/shard_map/all_to_all | solution.py:332
  394.7 0.6 copy-start.4
  395.3 0.6 copy-start.5

commit v3 on v2

--- a/solution.py
+++ b/solution.py
@@ -229,7 +229,7 @@
         kick_ref[q, 0] = jnp.where(live, vel_ref[q, 0] - slope, 0.0)
 
 
-def poisson(root_density):
+def poisson(root_density, beside_work):
     size_first = lax.axis_size("px")
     size_second = lax.axis_size("py")
     devices = size_first * size_second
@@ -247,6 +247,8 @@
     )
     f = jnp.einsum("yxz,cz->yxc", planes, basis, precision=HIGH)
     f = jnp.einsum("yxc,ax->yac", f, basis, precision=HIGH)
+    f, beside = lax.optimization_barrier((f, beside_work[0]))
+    beside = beside_work[1](*beside)
     tile = 48
     grid = NR // tile
     f_spec = pl.BlockSpec((rows, tile, NR), lambda t: (0, t, 0))
@@ -282,6 +284,7 @@
     )(got, lax.dynamic_slice_in_dim(eig_first, device * band, band, 0), eig_second)
     back = lax.all_to_all(carries, ("px", "py"), split_axis=0, concat_axis=0, tiled=True)
     back = back.reshape(devices, 2, band, NR).transpose(1, 0, 2, 3).reshape(2, NR, NR)
+    back, beside = lax.optimization_barrier((back, beside))
     whole_column = got[:, 2 * band, :rows].reshape(size_first, size_second, rows)
     whole_column = whole_column.transpose(1, 0, 2).reshape(NR)
     own = lax.dynamic_slice_in_dim(
@@ -299,8 +302,9 @@
     )(f, back, eig_first, eig_second, zero_wide)
     u = jnp.einsum("yac,ax->yxc", u, basis, precision=HIGH)
     u = jnp.einsum("yxc,cz->yxz", u, basis, precision=HIGH)
-    u = lax.all_to_all(u, "px", split_axis=1, concat_axis=0, tiled=True)
-    return jnp.transpose(u, (1, 0, 2))
+    u = u.reshape(rows, size_first, NR // size_first, NR).transpose(1, 0, 2, 3)
+    u = lax.all_to_all(u, "px", split_axis=0, concat_axis=0, tiled=True)
+    return u.reshape(size_first * rows, NR // size_first, NR), beside
 
 
 def local(root_density, subgrid_density, velocity, slot_anchor, slot_count, neighbour):
@@ -312,43 +316,52 @@
     per_device = subgrid_density.shape[0]
     side = EDGE * CELLS
     inner = CELLS * CELLS
-    low_density = from_behind(subgrid_density[:, :, inner - side :], "py", 1)
-    high_density = from_behind(subgrid_density[:, :, :side], "py", -1)
-    coarse_potential = poisson(root_density)
-    padded = extended(extended(coarse_potential, "px", 0, 1), "py", 1, 2)
-    patches = []
-    for target in range(size_second):
-        owner = place_first * size_second + target
-        wanted = (place_second - target) % size_second
-        anchor = slot_anchor[:, owner * per_device + wanted]
+    positions = jnp.arange(per_device, dtype=jnp.int32)
+
+    def early(density, anchors, counts, near):
+        low_density = from_behind(density[:, :, inner - side :], "py", 1)
+        high_density = from_behind(density[:, :, :side], "py", -1)
+        owner = place_first * size_second + jnp.arange(size_second, dtype=jnp.int32)
+        wanted = (place_second - jnp.arange(size_second, dtype=jnp.int32)) % size_second
+        anchor = anchors[:, owner * per_device + wanted]
         x = jnp.clip(anchor[0] - place_first * first_rows, 0, first_rows - REG)
         y = jnp.clip(anchor[1] - place_second * second_rows, 0, second_rows - REG)
-        cut = lax.dynamic_slice(padded, (x, y, 0), (PATCH_X, PATCH_Y, NR))
-        columns = (anchor[2] - 1 + jnp.arange(PATCH_Z, dtype=jnp.int32)) % NR
-        pick = (jnp.arange(NR, dtype=jnp.int32)[:, None] == columns[None, :]).astype(F32)
-        patches.append(
-            jnp.dot(cut.reshape(PATCH_X * PATCH_Y, NR), pick, precision=HIGHEST).reshape(-1)
-        )
+        columns = (anchor[2][:, None] - 1 + jnp.arange(PATCH_Z, dtype=jnp.int32)) % NR
+        pick = (jnp.arange(NR, dtype=jnp.int32)[None, :, None] == columns[:, None, :]).astype(F32)
+        slots = device * per_device + positions
+        below, above = near[0][slots], near[1][slots]
+        flags = jnp.stack(
+            [
+                positions < counts[device],
+                below >= 0,
+                above >= 0,
+                near[1][jnp.maximum(below, 0)] >= 0,
+                near[0][jnp.maximum(above, 0)] >= 0,
+            ]
+        ).astype(jnp.int32)
+        return low_density, high_density, x, y, pick, flags
+
+    held, (low_density, high_density, x, y, pick, flags) = poisson(
+        root_density, ((subgrid_density, slot_anchor, slot_count, neighbour), early)
+    )
+    coarse_potential = jnp.transpose(held, (1, 0, 2))
+    padded = extended(extended(held, "px", 1, 1), "py", 0, 2)
+    cuts = jnp.stack(
+        [
+            lax.dynamic_slice(padded, (y[t], x[t], 0), (PATCH_Y, PATCH_X, NR))
+            for t in range(size_second)
+        ]
+    )
+    patches = jnp.einsum("tyxn,tnz->txyz", cuts, pick, precision=HIGHEST)
+    patches = patches.reshape(size_second, -1)
     arrived = lax.all_to_all(
-        jnp.stack(patches), "py", split_axis=0, concat_axis=0, tiled=True
-    )
-    positions = jnp.arange(per_device, dtype=jnp.int32)
+        patches, "py", split_axis=0, concat_axis=0, tiled=True
+    )
     patch = arrived[(place_second + positions) % size_second]
     patch = patch.reshape(per_device, PATCH_X, PATCH_Y * PATCH_Z)
     patch = jnp.pad(
         patch, ((0, 0), (0, 16 - PATCH_X), (0, 128 - PATCH_Y * PATCH_Z))
     )
-    slots = device * per_device + positions
-    below, above = neighbour[0][slots], neighbour[1][slots]
-    flags = jnp.stack(
-        [
-            positions < slot_count[device],
-            below >= 0,
-            above >= 0,
-            neighbour[1][jnp.maximum(below, 0)] >= 0,
-            neighbour[0][jnp.maximum(above, 0)] >= 0,
-        ]
-    ).astype(jnp.int32)
     x_table, yz_table = patch_tables()
     slot_spec = lambda width: pl.BlockSpec((1, CELLS, width), lambda s: (s, 0, 0))
     vel_spec = pl.BlockSpec((3, 1, CELLS, inner), lambda s: (0, s, 0, 0))

time: 419 us -> 405 us (0.967)
  waiting for transfers between devices: 155 us -> 56.4 us
  blocking collectives: 83.1 us -> 165 us
  local copies, waits for them, and re-layouts: 57.1 us -> 39.7 us
  between operations: 16.7 us -> 31.6 us
  matrix products: 31.9 us -> 38.5 us
  starting transfers between devices: 27.8 us -> 22.8 us
    all_to_all x0 -> x1, blocking collectives: none -> 81.9 us  [poisson(): u = lax.all_to_all(u, 'px', split_axis=0, concat_axis=0, tiled=True)]
    all_to_all x2 -> x1, waiting for transfers between devices: 74.8 us -> 0.01 us  [local(): lax.all_to_all(patches, 'py', split_axis=0, concat_axis=0, tiled=True)]
    all_to_all x1, waiting for transfers between devices: 28.4 us -> 16.8 us  [poisson(): lax.all_to_all(carries, ('px', 'py'), split_axis=0, concat_axis=0, tiled=...]
    ppermute x2, waiting for transfers between devices: 12.3 us -> 2.14 us  [extended(): lax.ppermute(lax.slice_in_dim(block, block.shape[dim] - width, None, axis...]
    dot_general x1 -> x0, local copies, waits for them, and re-layouts: 7.82 us -> none  [poisson(): u = jnp.einsum('yxc,cz->yxz', u, basis, precision=HIGH)]
    dot_general x8 -> x1, matrix products: 2.24 us -> 9.21 us  [local(): patches = jnp.einsum('tyxn,tnz->txyz', cuts, pick, precision=HIGHEST)]
    all_to_all x2 -> x1, starting transfers between devices: 9.5 us -> 3.56 us  [local(): lax.all_to_all(patches, 'py', split_axis=0, concat_axis=0, tiled=True)]
    all_to_all x2 -> x1, local copies, waits for them, and re-layouts: 6.51 us -> 0.94 us  [local(): lax.all_to_all(patches, 'py', split_axis=0, concat_axis=0, tiled=True)]
  transfers between devices with their start and end apart: 10 -> 9, of which waited for: 6 -> 3; matrix products, arithmetic and copies ran while one was open for 9% -> 6% of each run, Pallas kernels for 0% -> 0%
where the time goes in v3:
time: 405 us; the launch traced here: 401 us
  blocking collectives  165 us (41%)
  waiting for transfers between devices  56.4 us (14%)
  local copies, waits for them, and re-layouts  39.7 us (10%)
  matrix products  38.5 us (10%)
  Pallas kernels  38.3 us (9%)
  between operations  31.6 us (8%)
  starting transfers between devices  22.8 us (6%)
  other arithmetic  8.55 us (2%)
    all_to_all x1, blocking collectives, poisson(): lax.all_to_all(jnp.transpose(root_density, (1, 0, 2)), 'px', split_axis=0...  83.1 us
    all_to_all x1, blocking collectives, poisson(): u = lax.all_to_all(u, 'px', split_axis=0, concat_axis=0, tiled=True)  81.9 us
    all_to_all x1, waiting for transfers between devices, poisson(): lax.all_to_all(sent, ('px', 'py'), split_axis=0, concat_axis=0, tiled=True)  37.4 us
    unnamed x28, local copies, waits for them, and re-layouts  20.4 us
    pallas_call x1, Pallas kernels, local(): pl.pallas_call(subgrid_kernel, grid=(per_device,), in_specs=[pl.BlockSpec...  18.6 us
    all_to_all x1, waiting for transfers between devices, poisson(): lax.all_to_all(carries, ('px', 'py'), split_axis=0, concat_axis=0, tiled=...  16.8 us
    pallas_call x1, Pallas kernels, poisson(): pl.pallas_call(solve_kernel, grid=(grid,), in_specs=[f_spec, pair_spec, e...  9.4 us
    dot_general x1, matrix products, local(): patches = jnp.einsum('tyxn,tnz->txyz', cuts, pick, precision=HIGHEST)  9.21 us
  transfers between devices with their start and end apart: 9, of which 3 were waited for; matrix products, arithmetic and copies ran while one was open for 6% of the time, Pallas kernels for 0%

profile of v3, /device:TPU:0, one launch (start us, length us, event | category | flops | bytes accessed | tf_op | source)
XLA Modules:
  0.0 400.9 jit_solution(14443892376528291641)
XLA Ops:
  0.6 5.3 %copy.110 = f32[96,48,384]{2,0,1:T(8,128)S(1)} copy(f32[96,48,384]{2,1,0:T(8,128)} %param.12) | data formatting | bytes 14155776 | tf_op args[0]
  5.9 83.1 %all_to_all.46 = f32[48,96,384]{2,1,0:T(8,128)S(1)} all-to-all(f32[48,96,384]{2,1,0:T(8,128)S(1)} %bitcast.116), channel_id=1, replica_groups=mesh['px'=4,'py'=8] {'px'}, dimensions={0} | all-to-all | bytes 14155776 | tf_op jit(solution)/shard_map/all_to_all | solution.py:245
  90.1 6.1 %fusion.23 = f32[384,12,384]{2,0,1:T(8,128)S(1)} fusion(f32[384,384,1]{1,0,2:T(8,128)S(1)} %copy-done.2, f32[12,384,384]{2,1,0:T(8,128)S(1)} %bitcast.113), kind=kOutput, calls=%fused_computation.83 | convolution fusion | flops 4076863488 | bytes 14745600 | tf_op jit(solution)/shard_map/yxz,cz->yxc/dot_general | solution.py:248
  96.2 6.2 %fusion.4.f_ref = f32[12,384,384]{2,1,0:T(8,128)S(1)} fusion(f32[384,384,1]{1,0,2:T(8,128)S(1)} %copy-done.2, f32[384,12,384]{2,0,1:T(8,128)S(1)} %fusion.23), kind=kOutput, calls=%fused_computation.13 | convolution fusion | flops 4076863488 | bytes 14745600 | tf_op jit(solution)/shard_map/yxc,ax->yac/dot_general | solution.py:249
  102.4 3.0 copy-done.1
  105.6 7.4 %shard_map.139 = f32[2,384,384]{2,1,0:T(8,128)} custom-call(f32[12,384,384]{2,1,0:T(8,128)} %copy-done.1, f32[384,1]{1,0:T(8,128)} %constant.83.clone.eb_ref, f32[1,384]{1,0:T(1,128)} %constant.84.clone.ec_ref.refs_2_), custom_call_target="tpu_custom_call" | custom-call | tf_op jit(solution)/shard_map/pallas_call | solution.py:261
  112.9 2.2 copy.70
  116.1 1.3 pad_maximum_fusion.1
  117.4 5.1 %all-to-all-start.1 = ((f32[32,32,384]{2,1,0:T(8,128)}), f32[32,32,384]{2,1,0:T(8,128)S(1)}, u32[]{:S(2)}, u32[]{:S(2)}) async-start(f32[32,32,384]{2,1,0:T(8,128)} %pad_maximum_fusion.1), calls=%async_computation.1 | async-start | bytes 3145728 | tf_op jit(solution)/shard_map/all_to_all | solution.py:279
  122.5 1.3 constant_dynamic-slice_fusion.8.refs_1_
  123.9 37.4 %all-to-all-done.1.refs_0_ = f32[32,32,384]{2,1,0:T(8,128)S(1)} async-done(((f32[32,32,384]{2,1,0:T(8,128)}), f32[32,32,384]{2,1,0:T(8,128)S(1)}, u32[]{:S(2)}, u32[]{:S(2)}) %all-to-all-start.1) | async-done | bytes 1572896 | tf_op jit(solution)/shard_map/all_to_all | solution.py:279
  161.2 1.1 copy-done.3
  162.4 2.9 shard_map.140
  165.3 2.8 all-to-all-start.2
  170.9 1.0 fusion.19
  171.9 3.6 collective-permute-start
  175.5 1.3 collective-permute-start.1
  181.6 16.8 %all-to-all-done.2 = f32[32,24,384]{2,1,0:T(8,128)S(1)} async-done(((f32[32,24,384]{2,1,0:T(8,128)}), f32[32,24,384]{2,1,0:T(8,128)S(1)}, u32[]{:S(2)}, u32[]{:S(2)}) %all-to-all-start.2) | async-done | bytes 1179680 | tf_op jit(solution)/shard_map/all_to_all | solution.py:285
  199.6 1.1 copy.77.carry_ref
  201.4 9.4 %shard_map.141 = f32[12,384,384]{2,1,0:T(8,128)} custom-call(f32[12,384,384]{2,1,0:T(8,128)} %copy-done.1, f32[2,384,384]{2,1,0:T(8,128)} %copy.77.carry_ref, f32[384,1]{1,0:T(8,128)} %constant.83.clone.eb_ref, f32[1,384]{1,0:T(1,128)} %constant.84.clone.ec_ref.refs_2_, f32[12,384]{1,0:T(8,128)} %broadcast_in_dim.5.zero_ref), custom_call_target="tpu_custom_call" | custom-call | tf_op jit(solution)/shard_map/pallas_call | solution.py:295
  210.8 9.2 %fusion.24 = f32[12,384,384]{2,1,0:T(8,128)S(1)} fusion(f32[12,384,384]{2,1,0:T(8,128)} %shard_map.141, f32[384,384,1]{1,0,2:T(8,128)S(1)} %copy-done.2), kind=kOutput, calls=%fused_computation.84 | convolution fusion | flops 4076863488 | bytes 14745600 | tf_op jit(solution)/shard_map/yac,ax->yxc/dot_general | solution.py:303
  220.0 7.8 %fusion = f32[12,384,384]{2,1,0:T(8,128)S(1)} fusion(f32[384,384,1]{1,0,2:T(8,128)S(1)} %copy-done.2, f32[12,384,384]{2,1,0:T(8,128)S(1)} %fusion.24), kind=kOutput, calls=%fused_computation.7 | convolution fusion | flops 4076863488 | bytes 14745600 | tf_op jit(solution)/shard_map/yxc,cz->yxz/dot_general | solution.py:304
  228.3 81.9 %all_to_all.47 = f32[4,12,96,384]{3,2,1,0:T(8,128)S(1)} all-to-all(f32[4,12,96,384]{3,2,1,0:T(8,128)S(1)} %bitcast.115), channel_id=1, replica_groups=mesh['px'=4,'py'=8] {'px'}, dimensions={0} | all-to-all | bytes 14155776 | tf_op jit(solution)/shard_map/all_to_all | solution.py:306
  310.4 1.7 collective-permute-start.3
  312.1 2.1 collective-permute-done.2
  315.1 4.0 collective-permute-start.5
  350.8 4.6 %pad_maximum_fusion = f32[52,98,384]{2,1,0:T(8,128)S(1)} fusion(f32[2,98,384]{2,1,0:T(8,128)S(1)} %collective-permute-done.5, f32[48,1,384]{2,1,0:T(1,128)S(1)} %collective-permute-done.3, f32[48,96,384]{2,1,0:T(8,128)} %bitcast.110, f32[48,1,384]{2,1,0:T(1,128)S(1)} %collective-permute-done.2, f32[2,98,384]{2,1,0:T(8,128)S(1)} %collective-permute-done.4), kind=kLoop, calls=%fused_computation.6 | loop fusion | flops 7827456 | bytes 15654912 | tf_op jit(solution)/shard_map/concatenate | solution.py:102
  356.3 9.2 %convolution_bitcast_fusion = f32[8,10,12,10]{2,3,1,0:T(8,128)S(1)} fusion(f32[8,12,10,384]{3,1,2,0:T(8,128)S(1)} %bitcast_dynamic-update-slice_fusion, f32[8,384,10]{1,2,0:T(8,128)S(1)} %fusion.8), kind=kOutput, calls=%fused_computation.15 | convolution fusion | flops 44236800 | bytes 1635840 | tf_op jit(solution)/shard_map/tyxn,tnz->txyz/dot_general | solution.py:355
  366.1 0.9 all_to_all.40
  367.1 3.6 all-to-all-start.4
  370.6 10.1 %copy.91 = f32[96,48,384]{2,1,0:T(8,128)} copy(f32[96,48,384]{2,0,1:T(8,128)} %bitcast.111) | data formatting | bytes 14155776
  382.0 18.6 %shard_map.142 = (f32[8,32,1024]{2,1,0:T(8,128)}, f32[3,8,32,1024]{3,2,1,0:T(8,128)}) custom-call(s32[5,8]{1,0:T(8,128)} %convert_element_type.11.flag_ref, f32[8,16,128]{2,1,0:T(8,128)} %pad.9.patch_ref, f32[40,16]{1,0:T(8,128)} %constant.86.clone.xt_ref, f32[128,3840]{1,0:T(8,128)} %constant.87.clone.yz_ref, f32[8,32,1024]{2,1,0:T(8,128)} %mid_ref.1, ...), custom_call_target="tpu_custom_call" | custom-call | tf_op jit(solution)/shard_map/pallas_call | solution.py:368
  (82 shorter events, 17.3 us)
Async XLA Ops:
  89.0 1.1 copy-start.2
  102.4 3.0 copy-start.1
  117.4 43.9 %all-to-all-start.1 = ((f32[32,32,384]{2,1,0:T(8,128)}), f32[32,32,384]{2,1,0:T(8,128)S(1)}, u32[]{:S(2)}, u32[]{:S(2)}) async-start(f32[32,32,384]{2,1,0:T(8,128)} %pad_maximum_fusion.1), calls=%async_computation.1 | async-start | bytes 3145728 | tf_op jit(solution)/shard_map/all_to_all | solution.py:279
  122.4 45.6 %copy-start.7 = (s32[2,256]{1,0:T(2,128)S(1)}, s32[2,256]{1,0:T(2,128)}, u32[]{:S(2)}) copy-start(s32[2,256]{1,0:T(2,128)} %param.17) | copy-start | bytes 6148
  123.8 46.9 %copy-start.6 = (s32[3,256]{1,0:T(4,128)S(1)}, s32[3,256]{1,0:T(4,128)}, u32[]{:S(2)}) copy-start(s32[3,256]{1,0:T(4,128)} %param.15) | copy-start | bytes 9220
  161.2 1.1 copy-start.3
  165.3 11.5 %copy-start.8 = (s32[32]{0:T(128)S(1)}, s32[32]{0:T(128)}, u32[]{:S(2)}) copy-start(s32[32]{0:T(128)} %param.16) | copy-start | bytes 388
  165.3 33.1 %all-to-all-start.2 = ((f32[32,24,384]{2,1,0:T(8,128)}), f32[32,24,384]{2,1,0:T(8,128)S(1)}, u32[]{:S(2)}, u32[]{:S(2)}) async-start(f32[32,24,384]{2,1,0:T(8,128)} %shard_map.140), calls=%async_computation.2 | async-start | bytes 2359296 | tf_op jit(solution)/shard_map/all_to_all | solution.py:285
  171.9 27.7 %collective-permute-start = (f32[8,32,128]{2,1,0:T(8,128)S(1)}, f32[8,32,128]{2,1,0:T(8,128)S(1)}, u32[]{:S(2)}, u32[]{:S(2)}) collective-permute-start(f32[8,32,128]{2,1,0:T(8,128)S(1)} %get-tuple-element.56), channel_id=1, source_target_pairs={{0,1},{1,2},{2,3},{3,4},{4,5},{5,6},{6,7},{8,9},{9,10},{10,11},{11... | collective-permute-start | bytes 393224 | tf_op jit(solution)/shard_map/ppermute | solution.py:91
  175.5 24.1 %collective-permute-start.1 = (f32[8,32,128]{2,1,0:T(8,128)S(1)}, f32[8,32,128]{2,1,0:T(8,128)S(1)}, u32[]{:S(2)}, u32[]{:S(2)}) collective-permute-start(f32[8,32,128]{2,1,0:T(8,128)S(1)} %get-tuple-element.55), channel_id=1, source_target_pairs={{1,0},{2,1},{3,2},{4,3},{5,4},{6,5},{7,6},{9,8},{10,9},{11,10},{12... | collective-permute-start | bytes 393224 | tf_op jit(solution)/shard_map/ppermute | solution.py:91
  199.6 11.2 %copy-start.4 = (f32[8,32,128]{2,1,0:T(8,128)}, f32[8,32,128]{2,1,0:T(8,128)S(1)}, u32[]{:S(2)}) copy-start(f32[8,32,128]{2,1,0:T(8,128)S(1)} %collective-permute-done.low_ref) | copy-start | bytes 393220
  199.6 11.2 %copy-start.5 = (f32[8,32,128]{2,1,0:T(8,128)}, f32[8,32,128]{2,1,0:T(8,128)S(1)}, u32[]{:S(2)}) copy-start(f32[8,32,128]{2,1,0:T(8,128)S(1)} %collective-permute-done.1.high_ref) | copy-start | bytes 393220
  310.2 4.1 %copy-start = (f32[4,12,96,384]{3,2,1,0:T(8,128)}, f32[4,12,96,384]{3,2,1,0:T(8,128)S(1)}, u32[]{:S(2)}) copy-start(f32[4,12,96,384]{3,2,1,0:T(8,128)S(1)} %all_to_all.47) | copy-start | bytes 21233668
  310.3 3.9 collective-permute-start.2
  310.4 3.9 collective-permute-start.3
  314.3 36.4 %collective-permute-start.4 = (f32[2,98,384]{2,1,0:T(8,128)S(1)}, f32[2,98,384]{2,1,0:T(8,128)S(1)}, u32[]{:S(2)}, u32[]{:S(2)}) collective-permute-start(f32[2,98,384]{2,1,0:T(8,128)S(1)} %get-tuple-element.51), channel_id=1, source_target_pairs={{0,1},{1,2},{2,3},{3,4},{4,5},{5,6},{6,7},{7,0},{8,9},{9,10},{10,1... | collective-permute-start | bytes 903176 | tf_op jit(solution)/shard_map/ppermute | solution.py:98
  315.1 35.7 %collective-permute-start.5 = (f32[2,98,384]{2,1,0:T(8,128)S(1)}, f32[2,98,384]{2,1,0:T(8,128)S(1)}, u32[]{:S(2)}, u32[]{:S(2)}) collective-permute-start(f32[2,98,384]{2,1,0:T(8,128)S(1)} %get-tuple-element.52), channel_id=1, source_target_pairs={{1,0},{2,1},{3,2},{4,3},{5,4},{6,5},{7,6},{0,7},{9,8},{10,9},{11,1... | collective-permute-start | bytes 903176 | tf_op jit(solution)/shard_map/ppermute | solution.py:101
  367.1 13.6 %all-to-all-start.4 = ((f32[8,1,1200]{2,1,0:T(1,128)}), f32[8,1,1200]{2,1,0:T(1,128)S(1)}, u32[]{:S(2)}, u32[]{:S(2)}) async-start(f32[8,1,1200]{2,1,0:T(1,128)} %all_to_all.40), calls=%async_computation.4 | async-start | bytes 81920 | tf_op jit(solution)/shard_map/all_to_all | solution.py:357
